TPU v7x, 512 devices: a whole 4x4x16 slice. The times are simulated.
512 devices in a mesh: space: 64 (over x_lo, z, core), iter: 8 (over y, x_hi).
Axes of the slice: x: 4 (x_hi: 2, x_lo: 2; x = x_hi * 2 + x_lo), y: 4, z: 16, core: 2. Of those that a mesh axis runs over, the one named last changes fastest.
Arguments:
- start_state: float32 [8, 2, 256, 128, 128], P('iter', None, 'space'), may hold values from -1 to 1
- prior_path: float32 [8, 5, 256, 128, 128], P('iter', None, 'space'), may hold values from -1 to 1
- wave_speed: float32 [256, 128, 128], P('space'), may hold values from 0.3 to 1
- kerr_coeff: float32 [256, 128, 128], P('space'), may hold values from 0.02 to 0.15
Outputs:
- final_state: float32 [8, 2, 256, 128, 128], P('iter', None, 'space')
All inputs are finite; a program needn't handle non-finite values.
Results may differ from a plain program's by a relative error of at most 0.00002.
Values sent between devices are 32-bit elements; how exact they have to be, the bound alone decides.
A program may use at most 64 MiB of HBM per device.

v0:
```python
import jax
import jax.numpy as jnp
from jax import lax
from jax.sharding import PartitionSpec as P

STEPS = 5
TICKS = 4


TIME_STEP_SQ = 0.12


def with_halo(block, sides, width):
    for axis, dim in sides:
        count = lax.axis_size(axis)
        forward = [(i, i + 1) for i in range(count - 1)]
        backward = [(target, source) for source, target in forward]
        low = lax.ppermute(
            lax.slice_in_dim(block, block.shape[dim] - width, None, axis=dim), axis, forward
        )
        high = lax.ppermute(lax.slice_in_dim(block, 0, width, axis=dim), axis, backward)
        block = jnp.concatenate([low, block, high], axis=dim)
    return block


def passed_along(block, axis, distance):
    devices = range(lax.axis_size(axis))
    route = [((i - distance) % len(devices), i) for i in devices]
    return lax.ppermute(block, axis, route)


def pad_axis(field, along_axis):
    widths = [(0, 0)] * field.ndim
    widths[along_axis % field.ndim] = (2, 2)
    return jnp.pad(field, widths)


def second_diff(padded, along_axis):
    axis_pos = along_axis % padded.ndim
    inner_size = padded.shape[axis_pos] - 4

    def planes(offset):
        return lax.slice_in_dim(padded, offset, offset + inner_size, axis=axis_pos)

    return (-planes(0) + 16.0 * planes(1) - 30.0 * planes(2) + 16.0 * planes(3) - planes(4)) / 12.0


def leap_step(previous, current, lower_rim, upper_rim, wave_speed, kerr_coeff, guide_field):
    column = jnp.concatenate([lower_rim, current, upper_rim], axis=current.ndim - 3)
    laplace = (
        second_diff(column, -3)
        + second_diff(pad_axis(current, -2), -2)
        + second_diff(pad_axis(current, -1), -1)
    )
    square = guide_field * guide_field
    nonlinear = 3.0 * square * current - 2.0 * square * guide_field
    return 2.0 * current - previous + TIME_STEP_SQ * (wave_speed * laplace - kerr_coeff * nonlinear)


def per_device(start_state, prior_path, wave_speed, kerr_coeff):
    previous = start_state[0, 0]
    current = start_state[0, 1]
    incoming = prior_path[0]
    extended = with_halo(incoming, (("space", 1),), 2)
    lower_all = extended[:, :2]
    upper_all = extended[:, -2:]
    for tick_index in range(TICKS):
        produced = []
        sending = tick_index + 1 < TICKS
        for step_index in range(STEPS):
            produced.append(current)
            fresh = leap_step(
                previous,
                current,
                lower_all[step_index],
                upper_all[step_index],
                wave_speed,
                kerr_coeff,
                incoming[step_index],
            )
            previous, current = (current, fresh)
        if sending:
            outgoing = jnp.stack(produced, 0)
            incoming = passed_along(outgoing, "iter", 1)
            extended = with_halo(incoming, (("space", 1),), 2)
            lower_all = extended[:, :2]
            upper_all = extended[:, -2:]
    return jnp.stack([previous, current], 0)[None]


def solution(mesh):
    return jax.shard_map(
        per_device,
        mesh=mesh,
        in_specs=(
            P("iter", None, "space", None, None),
            P("iter", None, "space", None, None),
            P("space", None, None),
            P("space", None, None),
        ),
        out_specs=P("iter", None, "space", None, None),
        check_vma=False,
    )
```

profile of v0, /device:TPU:227, one launch (start us, length us, event | category | flops | bytes accessed | tf_op | source)
XLA Modules:
  0.0 181.1 jit_solution(17230455595063799438)
XLA Ops:
  0.0 1.4 fusion.568
  1.4 5.3 %collective-permute-start = (f32[5,2,128,128]{3,2,1,0:T(8,128)S(1)}, f32[5,2,128,128]{3,2,1,0:T(8,128)S(1)}, u32[]{:S(2)}, u32[]{:S(2)}) collective-permute-start(f32[5,2,128,128]{3,2,1,0:T(8,128)S(1)} %get-tuple-element.39), channel_id=1, source_target_pairs={{0,8},{8,16},{16,24},{24,32},{32,40},{40,48},{48,56},{56,64},{64,7... | collective-permute-start | bytes 1966088 | tf_op jit(solution)/shard_map/ppermute | solution.py:18
  6.8 1.9 %collective-permute-start.1 = (f32[5,2,128,128]{3,2,1,0:T(8,128)S(1)}, f32[5,2,128,128]{3,2,1,0:T(8,128)S(1)}, u32[]{:S(2)}, u32[]{:S(2)}) collective-permute-start(f32[5,2,128,128]{3,2,1,0:T(8,128)S(1)} %get-tuple-element.40), channel_id=1, source_target_pairs={{8,0},{16,8},{24,16},{32,24},{40,32},{48,40},{56,48},{64,56},{72,6... | collective-permute-start | bytes 1966088 | tf_op jit(solution)/shard_map/ppermute | solution.py:21
  8.8 5.5 %collective-permute-done = f32[5,2,128,128]{3,2,1,0:T(8,128)S(1)} collective-permute-done((f32[5,2,128,128]{3,2,1,0:T(8,128)S(1)}, f32[5,2,128,128]{3,2,1,0:T(8,128)S(1)}, u32[]{:S(2)}, u32[]{:S(2)}) %collective-permute-start) | collective-permute-done | bytes 655392 | tf_op jit(solution)/shard_map/ppermute | solution.py:18
  14.3 5.6 %collective-permute-done.1 = f32[5,2,128,128]{3,2,1,0:T(8,128)S(1)} collective-permute-done((f32[5,2,128,128]{3,2,1,0:T(8,128)S(1)}, f32[5,2,128,128]{3,2,1,0:T(8,128)S(1)}, u32[]{:S(2)}, u32[]{:S(2)}) %collective-permute-start.1) | collective-permute-done | bytes 655392 | tf_op jit(solution)/shard_map/ppermute | solution.py:21
  21.8 3.8 %collective-permute-start.2 = (f32[5,4,128,128]{3,2,1,0:T(8,128)S(1)}, f32[5,4,128,128]{3,2,1,0:T(8,128)S(1)}, u32[]{:S(2)}, u32[]{:S(2)}) collective-permute-start(f32[5,4,128,128]{3,2,1,0:T(8,128)S(1)} %get-tuple-element.25), channel_id=1, source_target_pairs={{7,0},{0,1},{1,2},{2,3},{3,4},{4,5},{5,6},{6,7},{15,8},{8,9},{9,10... | collective-permute-start | bytes 3932168 | tf_op jit(solution)/shard_map/ppermute | solution.py:29
  25.5 28.6 %collective-permute-done.2 = f32[5,4,128,128]{3,2,1,0:T(8,128)S(1)} collective-permute-done((f32[5,4,128,128]{3,2,1,0:T(8,128)S(1)}, f32[5,4,128,128]{3,2,1,0:T(8,128)S(1)}, u32[]{:S(2)}, u32[]{:S(2)}) %collective-permute-start.2) | collective-permute-done | bytes 1310752 | tf_op jit(solution)/shard_map/ppermute | solution.py:29
  54.3 5.7 %collective-permute-start.3 = (f32[5,2,128,128]{3,2,1,0:T(8,128)S(1)}, f32[5,2,128,128]{3,2,1,0:T(8,128)S(1)}, u32[]{:S(2)}, u32[]{:S(2)}) collective-permute-start(f32[5,2,128,128]{3,2,1,0:T(8,128)S(1)} %get-tuple-element.37), channel_id=1, source_target_pairs={{0,8},{8,16},{16,24},{24,32},{32,40},{40,48},{48,56},{56,64},{64,7... | collective-permute-start | bytes 1966088 | tf_op jit(solution)/shard_map/ppermute | solution.py:18
  59.9 1.9 %collective-permute-start.4 = (f32[5,2,128,128]{3,2,1,0:T(8,128)S(1)}, f32[5,2,128,128]{3,2,1,0:T(8,128)S(1)}, u32[]{:S(2)}, u32[]{:S(2)}) collective-permute-start(f32[5,2,128,128]{3,2,1,0:T(8,128)S(1)} %get-tuple-element.38), channel_id=1, source_target_pairs={{8,0},{16,8},{24,16},{32,24},{40,32},{48,40},{56,48},{64,56},{72,6... | collective-permute-start | bytes 1966088 | tf_op jit(solution)/shard_map/ppermute | solution.py:21
  62.3 5.1 %collective-permute-done.3 = f32[5,2,128,128]{3,2,1,0:T(8,128)S(1)} collective-permute-done((f32[5,2,128,128]{3,2,1,0:T(8,128)S(1)}, f32[5,2,128,128]{3,2,1,0:T(8,128)S(1)}, u32[]{:S(2)}, u32[]{:S(2)}) %collective-permute-start.3) | collective-permute-done | bytes 655392 | tf_op jit(solution)/shard_map/ppermute | solution.py:18
  67.5 5.6 %collective-permute-done.4 = f32[5,2,128,128]{3,2,1,0:T(8,128)S(1)} collective-permute-done((f32[5,2,128,128]{3,2,1,0:T(8,128)S(1)}, f32[5,2,128,128]{3,2,1,0:T(8,128)S(1)}, u32[]{:S(2)}, u32[]{:S(2)}) %collective-permute-start.4) | collective-permute-done | bytes 655392 | tf_op jit(solution)/shard_map/ppermute | solution.py:21
  74.9 1.9 %collective-permute-start.5 = (f32[5,4,128,128]{3,2,1,0:T(8,128)S(1)}, f32[5,4,128,128]{3,2,1,0:T(8,128)S(1)}, u32[]{:S(2)}, u32[]{:S(2)}) collective-permute-start(f32[5,4,128,128]{3,2,1,0:T(8,128)S(1)} %get-tuple-element.15), channel_id=1, source_target_pairs={{7,0},{0,1},{1,2},{2,3},{3,4},{4,5},{5,6},{6,7},{15,8},{8,9},{9,10... | collective-permute-start | bytes 3932168 | tf_op jit(solution)/shard_map/ppermute | solution.py:29
  76.8 28.2 %collective-permute-done.5 = f32[5,4,128,128]{3,2,1,0:T(8,128)S(1)} collective-permute-done((f32[5,4,128,128]{3,2,1,0:T(8,128)S(1)}, f32[5,4,128,128]{3,2,1,0:T(8,128)S(1)}, u32[]{:S(2)}, u32[]{:S(2)}) %collective-permute-start.5) | collective-permute-done | bytes 1310752 | tf_op jit(solution)/shard_map/ppermute | solution.py:29
  105.1 7.2 %collective-permute-start.6 = (f32[5,2,128,128]{3,2,1,0:T(8,128)S(1)}, f32[5,2,128,128]{3,2,1,0:T(8,128)S(1)}, u32[]{:S(2)}, u32[]{:S(2)}) collective-permute-start(f32[5,2,128,128]{3,2,1,0:T(8,128)S(1)} %get-tuple-element.35), channel_id=1, source_target_pairs={{0,8},{8,16},{16,24},{24,32},{32,40},{40,48},{48,56},{56,64},{64,7... | collective-permute-start | bytes 1966088 | tf_op jit(solution)/shard_map/ppermute | solution.py:18
  112.4 1.9 %collective-permute-start.7 = (f32[5,2,128,128]{3,2,1,0:T(8,128)S(1)}, f32[5,2,128,128]{3,2,1,0:T(8,128)S(1)}, u32[]{:S(2)}, u32[]{:S(2)}) collective-permute-start(f32[5,2,128,128]{3,2,1,0:T(8,128)S(1)} %get-tuple-element.36), channel_id=1, source_target_pairs={{8,0},{16,8},{24,16},{32,24},{40,32},{48,40},{56,48},{64,56},{72,6... | collective-permute-start | bytes 1966088 | tf_op jit(solution)/shard_map/ppermute | solution.py:21
  114.8 5.1 %collective-permute-done.6 = f32[5,2,128,128]{3,2,1,0:T(8,128)S(1)} collective-permute-done((f32[5,2,128,128]{3,2,1,0:T(8,128)S(1)}, f32[5,2,128,128]{3,2,1,0:T(8,128)S(1)}, u32[]{:S(2)}, u32[]{:S(2)}) %collective-permute-start.6) | collective-permute-done | bytes 655392 | tf_op jit(solution)/shard_map/ppermute | solution.py:18
  120.0 5.6 %collective-permute-done.7 = f32[5,2,128,128]{3,2,1,0:T(8,128)S(1)} collective-permute-done((f32[5,2,128,128]{3,2,1,0:T(8,128)S(1)}, f32[5,2,128,128]{3,2,1,0:T(8,128)S(1)}, u32[]{:S(2)}, u32[]{:S(2)}) %collective-permute-start.7) | collective-permute-done | bytes 655392 | tf_op jit(solution)/shard_map/ppermute | solution.py:21
  127.4 1.9 %collective-permute-start.8 = (f32[5,4,128,128]{3,2,1,0:T(8,128)S(1)}, f32[5,4,128,128]{3,2,1,0:T(8,128)S(1)}, u32[]{:S(2)}, u32[]{:S(2)}) collective-permute-start(f32[5,4,128,128]{3,2,1,0:T(8,128)S(1)} %get-tuple-element.5), channel_id=1, source_target_pairs={{7,0},{0,1},{1,2},{2,3},{3,4},{4,5},{5,6},{6,7},{15,8},{8,9},{9,10... | collective-permute-start | bytes 3932168 | tf_op jit(solution)/shard_map/ppermute | solution.py:29
  129.3 27.0 %collective-permute-done.8 = f32[5,4,128,128]{3,2,1,0:T(8,128)S(1)} collective-permute-done((f32[5,4,128,128]{3,2,1,0:T(8,128)S(1)}, f32[5,4,128,128]{3,2,1,0:T(8,128)S(1)}, u32[]{:S(2)}, u32[]{:S(2)}) %collective-permute-start.8) | collective-permute-done | bytes 1310752 | tf_op jit(solution)/shard_map/ppermute | solution.py:29
  156.4 8.4 %collective-permute-start.9 = (f32[5,2,128,128]{3,2,1,0:T(8,128)S(1)}, f32[5,2,128,128]{3,2,1,0:T(8,128)S(1)}, u32[]{:S(2)}, u32[]{:S(2)}) collective-permute-start(f32[5,2,128,128]{3,2,1,0:T(8,128)S(1)} %get-tuple-element.33), channel_id=1, source_target_pairs={{0,8},{8,16},{16,24},{24,32},{32,40},{40,48},{48,56},{56,64},{64,7... | collective-permute-start | bytes 1966088 | tf_op jit(solution)/shard_map/ppermute | solution.py:18
  164.8 2.1 %collective-permute-start.10 = (f32[5,2,128,128]{3,2,1,0:T(8,128)S(1)}, f32[5,2,128,128]{3,2,1,0:T(8,128)S(1)}, u32[]{:S(2)}, u32[]{:S(2)}) collective-permute-start(f32[5,2,128,128]{3,2,1,0:T(8,128)S(1)} %get-tuple-element.34), channel_id=1, source_target_pairs={{8,0},{16,8},{24,16},{32,24},{40,32},{48,40},{56,48},{64,56},{72,6... | collective-permute-start | bytes 1966088 | tf_op jit(solution)/shard_map/ppermute | solution.py:21
  167.4 4.9 %collective-permute-done.9 = f32[5,2,128,128]{3,2,1,0:T(8,128)S(1)} collective-permute-done((f32[5,2,128,128]{3,2,1,0:T(8,128)S(1)}, f32[5,2,128,128]{3,2,1,0:T(8,128)S(1)}, u32[]{:S(2)}, u32[]{:S(2)}) %collective-permute-start.9) | collective-permute-done | bytes 655392 | tf_op jit(solution)/shard_map/ppermute | solution.py:18
  172.4 5.6 %collective-permute-done.10 = f32[5,2,128,128]{3,2,1,0:T(8,128)S(1)} collective-permute-done((f32[5,2,128,128]{3,2,1,0:T(8,128)S(1)}, f32[5,2,128,128]{3,2,1,0:T(8,128)S(1)}, u32[]{:S(2)}, u32[]{:S(2)}) %collective-permute-start.10) | collective-permute-done | bytes 655392 | tf_op jit(solution)/shard_map/ppermute | solution.py:21
  180.3 0.8 maximum_bitcast_fusion
  (41 shorter events, 9.8 us)
Async XLA Ops:
  0.0 8.7 %copy-start.3 = (f32[1,2,4,128,128]{4,3,2,1,0:T(8,128)S(1)}, f32[1,2,4,128,128]{4,3,2,1,0:T(8,128)}, u32[]{:S(2)}) copy-start(f32[1,2,4,128,128]{4,3,2,1,0:T(8,128)} %param.4) | copy-start | bytes 1572868
  1.4 12.8 %collective-permute-start = (f32[5,2,128,128]{3,2,1,0:T(8,128)S(1)}, f32[5,2,128,128]{3,2,1,0:T(8,128)S(1)}, u32[]{:S(2)}, u32[]{:S(2)}) collective-permute-start(f32[5,2,128,128]{3,2,1,0:T(8,128)S(1)} %get-tuple-element.39), channel_id=1, source_target_pairs={{0,8},{8,16},{16,24},{24,32},{32,40},{40,48},{48,56},{56,64},{64,7... | collective-permute-start | bytes 1966088 | tf_op jit(solution)/shard_map/ppermute | solution.py:18
  6.8 13.1 %collective-permute-start.1 = (f32[5,2,128,128]{3,2,1,0:T(8,128)S(1)}, f32[5,2,128,128]{3,2,1,0:T(8,128)S(1)}, u32[]{:S(2)}, u32[]{:S(2)}) collective-permute-start(f32[5,2,128,128]{3,2,1,0:T(8,128)S(1)} %get-tuple-element.40), channel_id=1, source_target_pairs={{8,0},{16,8},{24,16},{32,24},{40,32},{48,40},{56,48},{64,56},{72,6... | collective-permute-start | bytes 1966088 | tf_op jit(solution)/shard_map/ppermute | solution.py:21
  8.8 11.2 %copy-start = (f32[4,128,128]{2,1,0:T(8,128)S(1)}, f32[4,128,128]{2,1,0:T(8,128)}, u32[]{:S(2)}) copy-start(f32[4,128,128]{2,1,0:T(8,128)} %param.6) | copy-start | bytes 786436
  8.8 11.2 %copy-start.1 = (f32[4,128,128]{2,1,0:T(8,128)S(1)}, f32[4,128,128]{2,1,0:T(8,128)}, u32[]{:S(2)}) copy-start(f32[4,128,128]{2,1,0:T(8,128)} %param.7) | copy-start | bytes 786436
  8.8 11.2 %copy-start.2 = (f32[1,5,4,128,128]{4,3,2,1,0:T(8,128)S(1)}, f32[1,5,4,128,128]{4,3,2,1,0:T(8,128)}, u32[]{:S(2)}) copy-start(f32[1,5,4,128,128]{4,3,2,1,0:T(8,128)} %param.5) | copy-start | bytes 3932164
  21.8 32.4 %collective-permute-start.2 = (f32[5,4,128,128]{3,2,1,0:T(8,128)S(1)}, f32[5,4,128,128]{3,2,1,0:T(8,128)S(1)}, u32[]{:S(2)}, u32[]{:S(2)}) collective-permute-start(f32[5,4,128,128]{3,2,1,0:T(8,128)S(1)} %get-tuple-element.25), channel_id=1, source_target_pairs={{7,0},{0,1},{1,2},{2,3},{3,4},{4,5},{5,6},{6,7},{15,8},{8,9},{9,10... | collective-permute-start | bytes 3932168 | tf_op jit(solution)/shard_map/ppermute | solution.py:29
  54.3 13.2 %collective-permute-start.3 = (f32[5,2,128,128]{3,2,1,0:T(8,128)S(1)}, f32[5,2,128,128]{3,2,1,0:T(8,128)S(1)}, u32[]{:S(2)}, u32[]{:S(2)}) collective-permute-start(f32[5,2,128,128]{3,2,1,0:T(8,128)S(1)} %get-tuple-element.37), channel_id=1, source_target_pairs={{0,8},{8,16},{16,24},{24,32},{32,40},{40,48},{48,56},{56,64},{64,7... | collective-permute-start | bytes 1966088 | tf_op jit(solution)/shard_map/ppermute | solution.py:18
  59.9 13.1 %collective-permute-start.4 = (f32[5,2,128,128]{3,2,1,0:T(8,128)S(1)}, f32[5,2,128,128]{3,2,1,0:T(8,128)S(1)}, u32[]{:S(2)}, u32[]{:S(2)}) collective-permute-start(f32[5,2,128,128]{3,2,1,0:T(8,128)S(1)} %get-tuple-element.38), channel_id=1, source_target_pairs={{8,0},{16,8},{24,16},{32,24},{40,32},{48,40},{56,48},{64,56},{72,6... | collective-permute-start | bytes 1966088 | tf_op jit(solution)/shard_map/ppermute | solution.py:21
  74.9 30.1 %collective-permute-start.5 = (f32[5,4,128,128]{3,2,1,0:T(8,128)S(1)}, f32[5,4,128,128]{3,2,1,0:T(8,128)S(1)}, u32[]{:S(2)}, u32[]{:S(2)}) collective-permute-start(f32[5,4,128,128]{3,2,1,0:T(8,128)S(1)} %get-tuple-element.15), channel_id=1, source_target_pairs={{7,0},{0,1},{1,2},{2,3},{3,4},{4,5},{5,6},{6,7},{15,8},{8,9},{9,10... | collective-permute-start | bytes 3932168 | tf_op jit(solution)/shard_map/ppermute | solution.py:29
  105.1 14.8 %collective-permute-start.6 = (f32[5,2,128,128]{3,2,1,0:T(8,128)S(1)}, f32[5,2,128,128]{3,2,1,0:T(8,128)S(1)}, u32[]{:S(2)}, u32[]{:S(2)}) collective-permute-start(f32[5,2,128,128]{3,2,1,0:T(8,128)S(1)} %get-tuple-element.35), channel_id=1, source_target_pairs={{0,8},{8,16},{16,24},{24,32},{32,40},{40,48},{48,56},{56,64},{64,7... | collective-permute-start | bytes 1966088 | tf_op jit(solution)/shard_map/ppermute | solution.py:18
  112.4 13.1 %collective-permute-start.7 = (f32[5,2,128,128]{3,2,1,0:T(8,128)S(1)}, f32[5,2,128,128]{3,2,1,0:T(8,128)S(1)}, u32[]{:S(2)}, u32[]{:S(2)}) collective-permute-start(f32[5,2,128,128]{3,2,1,0:T(8,128)S(1)} %get-tuple-element.36), channel_id=1, source_target_pairs={{8,0},{16,8},{24,16},{32,24},{40,32},{48,40},{56,48},{64,56},{72,6... | collective-permute-start | bytes 1966088 | tf_op jit(solution)/shard_map/ppermute | solution.py:21
  127.4 28.9 %collective-permute-start.8 = (f32[5,4,128,128]{3,2,1,0:T(8,128)S(1)}, f32[5,4,128,128]{3,2,1,0:T(8,128)S(1)}, u32[]{:S(2)}, u32[]{:S(2)}) collective-permute-start(f32[5,4,128,128]{3,2,1,0:T(8,128)S(1)} %get-tuple-element.5), channel_id=1, source_target_pairs={{7,0},{0,1},{1,2},{2,3},{3,4},{4,5},{5,6},{6,7},{15,8},{8,9},{9,10... | collective-permute-start | bytes 3932168 | tf_op jit(solution)/shard_map/ppermute | solution.py:29
  156.4 15.9 %collective-permute-start.9 = (f32[5,2,128,128]{3,2,1,0:T(8,128)S(1)}, f32[5,2,128,128]{3,2,1,0:T(8,128)S(1)}, u32[]{:S(2)}, u32[]{:S(2)}) collective-permute-start(f32[5,2,128,128]{3,2,1,0:T(8,128)S(1)} %get-tuple-element.33), channel_id=1, source_target_pairs={{0,8},{8,16},{16,24},{24,32},{32,40},{40,48},{48,56},{56,64},{64,7... | collective-permute-start | bytes 1966088 | tf_op jit(solution)/shard_map/ppermute | solution.py:18
  164.8 13.1 %collective-permute-start.10 = (f32[5,2,128,128]{3,2,1,0:T(8,128)S(1)}, f32[5,2,128,128]{3,2,1,0:T(8,128)S(1)}, u32[]{:S(2)}, u32[]{:S(2)}) collective-permute-start(f32[5,2,128,128]{3,2,1,0:T(8,128)S(1)} %get-tuple-element.34), channel_id=1, source_target_pairs={{8,0},{16,8},{24,16},{32,24},{40,32},{48,40},{56,48},{64,56},{72,6... | collective-permute-start | bytes 1966088 | tf_op jit(solution)/shard_map/ppermute | solution.py:21
where the time goes:
time: 182 us; the launch traced here: 181 us
  waiting for transfers between devices  127 us (70%)
  starting transfers between devices  42.1 us (23%)
  other arithmetic  9.87 us (5%)
  local copies, waits for them, and re-layouts  2.15 us (1%)
    ppermute x3, waiting for transfers between devices, passed_along(): return lax.ppermute(block, axis, route)  83.8 us
    ppermute x4, starting transfers between devices, with_halo(): lax.ppermute(lax.slice_in_dim(block, block.shape[dim] - width, None, axis...  26.6 us
    ppermute x4, waiting for transfers between devices, with_halo(): lax.ppermute(lax.slice_in_dim(block, 0, width, axis=dim), axis, backward)  22.2 us
    ppermute x4, waiting for transfers between devices, with_halo(): lax.ppermute(lax.slice_in_dim(block, block.shape[dim] - width, None, axis...  20.7 us
    ppermute x4, starting transfers between devices, with_halo(): lax.ppermute(lax.slice_in_dim(block, 0, width, axis=dim), axis, backward)  7.86 us
    ppermute x3, starting transfers between devices, passed_along(): return lax.ppermute(block, axis, route)  7.59 us
    unnamed x11, other arithmetic  4.96 us
  transfers between devices with their start and end apart: 11, of which 11 were waited for; matrix products, arithmetic and copies ran while one was open for 1% of the time, Pallas kernels for 0%

commit v1 on v0

v1 whole, which is shorter than its diff:
```python
import jax
import jax.numpy as jnp
from jax import lax
from jax.sharding import PartitionSpec as P

STEPS = 5
TICKS = 4
TIME_STEP_SQ = 0.12


def halo_of(path):
    count = lax.axis_size("space")
    forward = [(i, i + 1) for i in range(count - 1)]
    backward = [(t, s) for s, t in forward]
    low = lax.ppermute(path[:, -2:], "space", forward)
    high = lax.ppermute(path[:, :2], "space", backward)
    return low, high


def shift_lanes(block, distance):
    n = lax.axis_size("iter")
    return lax.ppermute(block, "iter", [(i, (i + distance) % n) for i in range(n)])


def pad_axis(field, along_axis):
    widths = [(0, 0)] * field.ndim
    widths[along_axis % field.ndim] = (2, 2)
    return jnp.pad(field, widths)


def second_diff(padded, along_axis):
    axis_pos = along_axis % padded.ndim
    inner_size = padded.shape[axis_pos] - 4

    def planes(offset):
        return lax.slice_in_dim(padded, offset, offset + inner_size, axis=axis_pos)

    return (-planes(0) + 16.0 * planes(1) - 30.0 * planes(2) + 16.0 * planes(3) - planes(4)) / 12.0


def leap_step(previous, current, lower_rim, upper_rim, wave_speed, kerr_coeff, guide_field):
    column = jnp.concatenate([lower_rim, current, upper_rim], axis=current.ndim - 3)
    laplace = (
        second_diff(column, -3)
        + second_diff(pad_axis(current, -2), -2)
        + second_diff(pad_axis(current, -1), -1)
    )
    square = guide_field * guide_field
    nonlinear = 3.0 * square * current - 2.0 * square * guide_field
    return 2.0 * current - previous + TIME_STEP_SQ * (wave_speed * laplace - kerr_coeff * nonlinear)


def per_device(start_state, prior_path, wave_speed, kerr_coeff):
    state = start_state[0]
    incoming = prior_path[0]
    low, high = halo_of(incoming)
    for tick in range(TICKS):
        previous, current = state[0], state[1]
        produced = []
        for n in range(STEPS):
            produced.append(current)
            fresh = leap_step(previous, current, low[n], high[n], wave_speed, kerr_coeff, incoming[n])
            previous, current = current, fresh
        state = jnp.stack([previous, current], 0)
        if tick + 1 < TICKS:
            incoming = jnp.stack(produced, 0)
            low, high = halo_of(incoming)
            state = shift_lanes(state, -1)
    return shift_lanes(state, TICKS - 1)[None]


def solution(mesh):
    return jax.shard_map(
        per_device,
        mesh=mesh,
        in_specs=(
            P("iter", None, "space", None, None),
            P("iter", None, "space", None, None),
            P("space", None, None),
            P("space", None, None),
        ),
        out_specs=P("iter", None, "space", None, None),
        check_vma=False,
    )
```

time: 182 us -> 111 us (0.61)
  the two profiles are of different devices: /device:TPU:227 before, /device:TPU:2 now
where the time goes in v1:
time: 111 us
  starting transfers between devices  53.3 us (48%)
  waiting for transfers between devices  44.9 us (40%)
  other arithmetic  9.2 us (8%)
  local copies, waits for them, and re-layouts  3 us (3%)
    ppermute x4, starting transfers between devices, halo_of(): high = lax.ppermute(path[:, :2], 'space', backward)  30 us
    ppermute x4, waiting for transfers between devices, halo_of(): low = lax.ppermute(path[:, -2:], 'space', forward)  23.3 us
    ppermute x4, starting transfers between devices, shift_lanes(): lax.ppermute(block, 'iter', [(i, (i + distance) % n) for i in range(n)])  15.7 us
    ppermute x4, waiting for transfers between devices, shift_lanes(): lax.ppermute(block, 'iter', [(i, (i + distance) % n) for i in range(n)])  14.9 us
    ppermute x4, starting transfers between devices, halo_of(): low = lax.ppermute(path[:, -2:], 'space', forward)  7.68 us
    ppermute x4, waiting for transfers between devices, halo_of(): high = lax.ppermute(path[:, :2], 'space', backward)  6.71 us
    unnamed x9, other arithmetic  4.06 us
  transfers between devices with their start and end apart: 12, of which 10 were waited for; matrix products, arithmetic and copies ran while one was open for 1% of the time, Pallas kernels for 0%

profile of v1, /device:TPU:2, one launch (start us, length us, event | category | flops | bytes accessed | tf_op | source)
XLA Modules:
  0.0 110.8 jit_solution(3462184394664593200)
XLA Ops:
  0.0 1.4 %fusion.572 = (f32[5,2,128,128]{3,2,1,0:T(8,128)S(1)}, f32[5,2,128,128]{3,2,1,0:T(8,128)S(1)}) fusion(f32[5,4,128,128]{3,2,1,0:T(8,128)} %bitcast.228), kind=kLoop, calls=%fused_computation.877 | loop fusion | bytes 2621440 | tf_op jit(solution)/shard_map/slice | solution.py:15
  1.4 1.9 %collective-permute-start = (f32[5,2,128,128]{3,2,1,0:T(8,128)S(1)}, f32[5,2,128,128]{3,2,1,0:T(8,128)S(1)}, u32[]{:S(2)}, u32[]{:S(2)}) collective-permute-start(f32[5,2,128,128]{3,2,1,0:T(8,128)S(1)} %get-tuple-element.35), channel_id=1, source_target_pairs={{0,8},{8,16},{16,24},{24,32},{32,40},{40,48},{48,56},{56,64},{64,7... | collective-permute-start | bytes 1966088 | tf_op jit(solution)/shard_map/ppermute | solution.py:15
  3.4 10.8 %collective-permute-start.1 = (f32[5,2,128,128]{3,2,1,0:T(8,128)S(1)}, f32[5,2,128,128]{3,2,1,0:T(8,128)S(1)}, u32[]{:S(2)}, u32[]{:S(2)}) collective-permute-start(f32[5,2,128,128]{3,2,1,0:T(8,128)S(1)} %get-tuple-element.36), channel_id=1, source_target_pairs={{8,0},{16,8},{24,16},{32,24},{40,32},{48,40},{56,48},{64,56},{72,6... | collective-permute-start | bytes 1966088 | tf_op jit(solution)/shard_map/ppermute | solution.py:16
  14.3 6.2 %collective-permute-done = f32[5,2,128,128]{3,2,1,0:T(8,128)S(1)} collective-permute-done((f32[5,2,128,128]{3,2,1,0:T(8,128)S(1)}, f32[5,2,128,128]{3,2,1,0:T(8,128)S(1)}, u32[]{:S(2)}, u32[]{:S(2)}) %collective-permute-start) | collective-permute-done | bytes 655392 | tf_op jit(solution)/shard_map/ppermute | solution.py:15
  20.6 1.7 %collective-permute-done.1 = f32[5,2,128,128]{3,2,1,0:T(8,128)S(1)} collective-permute-done((f32[5,2,128,128]{3,2,1,0:T(8,128)S(1)}, f32[5,2,128,128]{3,2,1,0:T(8,128)S(1)}, u32[]{:S(2)}, u32[]{:S(2)}) %collective-permute-start.1) | collective-permute-done | bytes 655392 | tf_op jit(solution)/shard_map/ppermute | solution.py:16
  24.7 6.8 %collective-permute-start.2 = (f32[2,4,128,128]{3,2,1,0:T(8,128)S(1)}, f32[2,4,128,128]{3,2,1,0:T(8,128)S(1)}, u32[]{:S(2)}, u32[]{:S(2)}) collective-permute-start(f32[2,4,128,128]{3,2,1,0:T(8,128)S(1)} %pad_maximum_fusion), channel_id=1, source_target_pairs={{0,7},{1,0},{2,1},{3,2},{4,3},{5,4},{6,5},{7,6},{8,15},{9,8},{10,9... | collective-permute-start | bytes 1572872 | tf_op jit(solution)/shard_map/ppermute | solution.py:22
  31.6 1.9 %collective-permute-start.3 = (f32[5,2,128,128]{3,2,1,0:T(8,128)S(1)}, f32[5,2,128,128]{3,2,1,0:T(8,128)S(1)}, u32[]{:S(2)}, u32[]{:S(2)}) collective-permute-start(f32[5,2,128,128]{3,2,1,0:T(8,128)S(1)} %get-tuple-element.33), channel_id=1, source_target_pairs={{0,8},{8,16},{16,24},{24,32},{32,40},{40,48},{48,56},{56,64},{64,7... | collective-permute-start | bytes 1966088 | tf_op jit(solution)/shard_map/ppermute | solution.py:15
  33.5 6.3 %collective-permute-start.4 = (f32[5,2,128,128]{3,2,1,0:T(8,128)S(1)}, f32[5,2,128,128]{3,2,1,0:T(8,128)S(1)}, u32[]{:S(2)}, u32[]{:S(2)}) collective-permute-start(f32[5,2,128,128]{3,2,1,0:T(8,128)S(1)} %get-tuple-element.34), channel_id=1, source_target_pairs={{8,0},{16,8},{24,16},{32,24},{40,32},{48,40},{56,48},{64,56},{72,6... | collective-permute-start | bytes 1966088 | tf_op jit(solution)/shard_map/ppermute | solution.py:16
  39.9 6.4 %collective-permute-done.3 = f32[5,2,128,128]{3,2,1,0:T(8,128)S(1)} collective-permute-done((f32[5,2,128,128]{3,2,1,0:T(8,128)S(1)}, f32[5,2,128,128]{3,2,1,0:T(8,128)S(1)}, u32[]{:S(2)}, u32[]{:S(2)}) %collective-permute-start.3) | collective-permute-done | bytes 655392 | tf_op jit(solution)/shard_map/ppermute | solution.py:15
  46.3 1.6 %collective-permute-done.4 = f32[5,2,128,128]{3,2,1,0:T(8,128)S(1)} collective-permute-done((f32[5,2,128,128]{3,2,1,0:T(8,128)S(1)}, f32[5,2,128,128]{3,2,1,0:T(8,128)S(1)}, u32[]{:S(2)}, u32[]{:S(2)}) %collective-permute-start.4) | collective-permute-done | bytes 655392 | tf_op jit(solution)/shard_map/ppermute | solution.py:16
  50.3 2.4 %collective-permute-start.5 = (f32[2,4,128,128]{3,2,1,0:T(8,128)S(1)}, f32[2,4,128,128]{3,2,1,0:T(8,128)S(1)}, u32[]{:S(2)}, u32[]{:S(2)}) collective-permute-start(f32[2,4,128,128]{3,2,1,0:T(8,128)S(1)} %pad_maximum_fusion.1), channel_id=1, source_target_pairs={{0,7},{1,0},{2,1},{3,2},{4,3},{5,4},{6,5},{7,6},{8,15},{9,8},{10,9... | collective-permute-start | bytes 1572872 | tf_op jit(solution)/shard_map/ppermute | solution.py:22
  52.9 1.9 %collective-permute-start.6 = (f32[5,2,128,128]{3,2,1,0:T(8,128)S(1)}, f32[5,2,128,128]{3,2,1,0:T(8,128)S(1)}, u32[]{:S(2)}, u32[]{:S(2)}) collective-permute-start(f32[5,2,128,128]{3,2,1,0:T(8,128)S(1)} %get-tuple-element.31), channel_id=1, source_target_pairs={{0,8},{8,16},{16,24},{24,32},{32,40},{40,48},{48,56},{56,64},{64,7... | collective-permute-start | bytes 1966088 | tf_op jit(solution)/shard_map/ppermute | solution.py:15
  54.8 6.3 %collective-permute-start.7 = (f32[5,2,128,128]{3,2,1,0:T(8,128)S(1)}, f32[5,2,128,128]{3,2,1,0:T(8,128)S(1)}, u32[]{:S(2)}, u32[]{:S(2)}) collective-permute-start(f32[5,2,128,128]{3,2,1,0:T(8,128)S(1)} %get-tuple-element.32), channel_id=1, source_target_pairs={{8,0},{16,8},{24,16},{32,24},{40,32},{48,40},{56,48},{64,56},{72,6... | collective-permute-start | bytes 1966088 | tf_op jit(solution)/shard_map/ppermute | solution.py:16
  61.1 1.8 %collective-permute-done.5 = f32[2,4,128,128]{3,2,1,0:T(8,128)S(1)} collective-permute-done((f32[2,4,128,128]{3,2,1,0:T(8,128)S(1)}, f32[2,4,128,128]{3,2,1,0:T(8,128)S(1)}, u32[]{:S(2)}, u32[]{:S(2)}) %collective-permute-start.5) | collective-permute-done | bytes 524320 | tf_op jit(solution)/shard_map/ppermute | solution.py:22
  62.9 4.5 %collective-permute-done.6 = f32[5,2,128,128]{3,2,1,0:T(8,128)S(1)} collective-permute-done((f32[5,2,128,128]{3,2,1,0:T(8,128)S(1)}, f32[5,2,128,128]{3,2,1,0:T(8,128)S(1)}, u32[]{:S(2)}, u32[]{:S(2)}) %collective-permute-start.6) | collective-permute-done | bytes 655392 | tf_op jit(solution)/shard_map/ppermute | solution.py:15
  67.5 1.7 %collective-permute-done.7 = f32[5,2,128,128]{3,2,1,0:T(8,128)S(1)} collective-permute-done((f32[5,2,128,128]{3,2,1,0:T(8,128)S(1)}, f32[5,2,128,128]{3,2,1,0:T(8,128)S(1)}, u32[]{:S(2)}, u32[]{:S(2)}) %collective-permute-start.7) | collective-permute-done | bytes 655392 | tf_op jit(solution)/shard_map/ppermute | solution.py:16
  71.5 4.6 %collective-permute-start.8 = (f32[2,4,128,128]{3,2,1,0:T(8,128)S(1)}, f32[2,4,128,128]{3,2,1,0:T(8,128)S(1)}, u32[]{:S(2)}, u32[]{:S(2)}) collective-permute-start(f32[2,4,128,128]{3,2,1,0:T(8,128)S(1)} %pad_maximum_fusion.2), channel_id=1, source_target_pairs={{0,7},{1,0},{2,1},{3,2},{4,3},{5,4},{6,5},{7,6},{8,15},{9,8},{10,9... | collective-permute-start | bytes 1572872 | tf_op jit(solution)/shard_map/ppermute | solution.py:22
  76.2 1.9 %collective-permute-start.9 = (f32[5,2,128,128]{3,2,1,0:T(8,128)S(1)}, f32[5,2,128,128]{3,2,1,0:T(8,128)S(1)}, u32[]{:S(2)}, u32[]{:S(2)}) collective-permute-start(f32[5,2,128,128]{3,2,1,0:T(8,128)S(1)} %get-tuple-element.29), channel_id=1, source_target_pairs={{0,8},{8,16},{16,24},{24,32},{32,40},{40,48},{48,56},{56,64},{64,7... | collective-permute-start | bytes 1966088 | tf_op jit(solution)/shard_map/ppermute | solution.py:15
  78.2 6.5 %collective-permute-start.10 = (f32[5,2,128,128]{3,2,1,0:T(8,128)S(1)}, f32[5,2,128,128]{3,2,1,0:T(8,128)S(1)}, u32[]{:S(2)}, u32[]{:S(2)}) collective-permute-start(f32[5,2,128,128]{3,2,1,0:T(8,128)S(1)} %get-tuple-element.30), channel_id=1, source_target_pairs={{8,0},{16,8},{24,16},{32,24},{40,32},{48,40},{56,48},{64,56},{72,6... | collective-permute-start | bytes 1966088 | tf_op jit(solution)/shard_map/ppermute | solution.py:16
  84.7 6.2 %collective-permute-done.9 = f32[5,2,128,128]{3,2,1,0:T(8,128)S(1)} collective-permute-done((f32[5,2,128,128]{3,2,1,0:T(8,128)S(1)}, f32[5,2,128,128]{3,2,1,0:T(8,128)S(1)}, u32[]{:S(2)}, u32[]{:S(2)}) %collective-permute-start.9) | collective-permute-done | bytes 655392 | tf_op jit(solution)/shard_map/ppermute | solution.py:15
  91.0 1.6 %collective-permute-done.10 = f32[5,2,128,128]{3,2,1,0:T(8,128)S(1)} collective-permute-done((f32[5,2,128,128]{3,2,1,0:T(8,128)S(1)}, f32[5,2,128,128]{3,2,1,0:T(8,128)S(1)}, u32[]{:S(2)}, u32[]{:S(2)}) %collective-permute-start.10) | collective-permute-done | bytes 655392 | tf_op jit(solution)/shard_map/ppermute | solution.py:16
  95.0 1.9 %collective-permute-start.11 = (f32[2,4,128,128]{3,2,1,0:T(8,128)S(1)}, f32[2,4,128,128]{3,2,1,0:T(8,128)S(1)}, u32[]{:S(2)}, u32[]{:S(2)}) collective-permute-start(f32[2,4,128,128]{3,2,1,0:T(8,128)S(1)} %pad_maximum_fusion.3), channel_id=1, source_target_pairs={{0,3},{1,4},{2,5},{3,6},{4,7},{5,0},{6,1},{7,2},{8,11},{9,12},{10,... | collective-permute-start | bytes 1572872 | tf_op jit(solution)/shard_map/ppermute | solution.py:22
  96.9 13.1 %collective-permute-done.11 = f32[2,4,128,128]{3,2,1,0:T(8,128)S(1)} collective-permute-done((f32[2,4,128,128]{3,2,1,0:T(8,128)S(1)}, f32[2,4,128,128]{3,2,1,0:T(8,128)S(1)}, u32[]{:S(2)}, u32[]{:S(2)}) %collective-permute-start.11) | collective-permute-done | bytes 524320 | tf_op jit(solution)/shard_map/ppermute | solution.py:22
  110.0 0.8 copy.18
  (50 shorter events, 10.0 us)
Async XLA Ops:
  0.0 14.2 %copy-start.3 = (f32[1,2,4,128,128]{4,3,2,1,0:T(8,128)S(1)}, f32[1,2,4,128,128]{4,3,2,1,0:T(8,128)}, u32[]{:S(2)}) copy-start(f32[1,2,4,128,128]{4,3,2,1,0:T(8,128)} %param.4) | copy-start | bytes 1572868
  1.4 19.1 %collective-permute-start = (f32[5,2,128,128]{3,2,1,0:T(8,128)S(1)}, f32[5,2,128,128]{3,2,1,0:T(8,128)S(1)}, u32[]{:S(2)}, u32[]{:S(2)}) collective-permute-start(f32[5,2,128,128]{3,2,1,0:T(8,128)S(1)} %get-tuple-element.35), channel_id=1, source_target_pairs={{0,8},{8,16},{16,24},{24,32},{32,40},{40,48},{48,56},{56,64},{64,7... | collective-permute-start | bytes 1966088 | tf_op jit(solution)/shard_map/ppermute | solution.py:15
  3.4 18.9 %collective-permute-start.1 = (f32[5,2,128,128]{3,2,1,0:T(8,128)S(1)}, f32[5,2,128,128]{3,2,1,0:T(8,128)S(1)}, u32[]{:S(2)}, u32[]{:S(2)}) collective-permute-start(f32[5,2,128,128]{3,2,1,0:T(8,128)S(1)} %get-tuple-element.36), channel_id=1, source_target_pairs={{8,0},{16,8},{24,16},{32,24},{40,32},{48,40},{56,48},{64,56},{72,6... | collective-permute-start | bytes 1966088 | tf_op jit(solution)/shard_map/ppermute | solution.py:16
  14.3 8.1 %copy-start = (f32[4,128,128]{2,1,0:T(8,128)S(1)}, f32[4,128,128]{2,1,0:T(8,128)}, u32[]{:S(2)}) copy-start(f32[4,128,128]{2,1,0:T(8,128)} %param.6) | copy-start | bytes 786436
  14.3 8.1 %copy-start.1 = (f32[4,128,128]{2,1,0:T(8,128)S(1)}, f32[4,128,128]{2,1,0:T(8,128)}, u32[]{:S(2)}) copy-start(f32[4,128,128]{2,1,0:T(8,128)} %param.7) | copy-start | bytes 786436
  14.3 8.1 %copy-start.2 = (f32[1,5,4,128,128]{4,3,2,1,0:T(8,128)S(1)}, f32[1,5,4,128,128]{4,3,2,1,0:T(8,128)}, u32[]{:S(2)}) copy-start(f32[1,5,4,128,128]{4,3,2,1,0:T(8,128)} %param.5) | copy-start | bytes 3932164
  24.7 15.2 %collective-permute-start.2 = (f32[2,4,128,128]{3,2,1,0:T(8,128)S(1)}, f32[2,4,128,128]{3,2,1,0:T(8,128)S(1)}, u32[]{:S(2)}, u32[]{:S(2)}) collective-permute-start(f32[2,4,128,128]{3,2,1,0:T(8,128)S(1)} %pad_maximum_fusion), channel_id=1, source_target_pairs={{0,7},{1,0},{2,1},{3,2},{4,3},{5,4},{6,5},{7,6},{8,15},{9,8},{10,9... | collective-permute-start | bytes 1572872 | tf_op jit(solution)/shard_map/ppermute | solution.py:22
  31.6 14.7 %collective-permute-start.3 = (f32[5,2,128,128]{3,2,1,0:T(8,128)S(1)}, f32[5,2,128,128]{3,2,1,0:T(8,128)S(1)}, u32[]{:S(2)}, u32[]{:S(2)}) collective-permute-start(f32[5,2,128,128]{3,2,1,0:T(8,128)S(1)} %get-tuple-element.33), channel_id=1, source_target_pairs={{0,8},{8,16},{16,24},{24,32},{32,40},{40,48},{48,56},{56,64},{64,7... | collective-permute-start | bytes 1966088 | tf_op jit(solution)/shard_map/ppermute | solution.py:15
  33.5 14.5 %collective-permute-start.4 = (f32[5,2,128,128]{3,2,1,0:T(8,128)S(1)}, f32[5,2,128,128]{3,2,1,0:T(8,128)S(1)}, u32[]{:S(2)}, u32[]{:S(2)}) collective-permute-start(f32[5,2,128,128]{3,2,1,0:T(8,128)S(1)} %get-tuple-element.34), channel_id=1, source_target_pairs={{8,0},{16,8},{24,16},{32,24},{40,32},{48,40},{56,48},{64,56},{72,6... | collective-permute-start | bytes 1966088 | tf_op jit(solution)/shard_map/ppermute | solution.py:16
  50.3 12.6 %collective-permute-start.5 = (f32[2,4,128,128]{3,2,1,0:T(8,128)S(1)}, f32[2,4,128,128]{3,2,1,0:T(8,128)S(1)}, u32[]{:S(2)}, u32[]{:S(2)}) collective-permute-start(f32[2,4,128,128]{3,2,1,0:T(8,128)S(1)} %pad_maximum_fusion.1), channel_id=1, source_target_pairs={{0,7},{1,0},{2,1},{3,2},{4,3},{5,4},{6,5},{7,6},{8,15},{9,8},{10,9... | collective-permute-start | bytes 1572872 | tf_op jit(solution)/shard_map/ppermute | solution.py:22
  52.9 14.6 %collective-permute-start.6 = (f32[5,2,128,128]{3,2,1,0:T(8,128)S(1)}, f32[5,2,128,128]{3,2,1,0:T(8,128)S(1)}, u32[]{:S(2)}, u32[]{:S(2)}) collective-permute-start(f32[5,2,128,128]{3,2,1,0:T(8,128)S(1)} %get-tuple-element.31), channel_id=1, source_target_pairs={{0,8},{8,16},{16,24},{24,32},{32,40},{40,48},{48,56},{56,64},{64,7... | collective-permute-start | bytes 1966088 | tf_op jit(solution)/shard_map/ppermute | solution.py:15
  54.8 14.4 %collective-permute-start.7 = (f32[5,2,128,128]{3,2,1,0:T(8,128)S(1)}, f32[5,2,128,128]{3,2,1,0:T(8,128)S(1)}, u32[]{:S(2)}, u32[]{:S(2)}) collective-permute-start(f32[5,2,128,128]{3,2,1,0:T(8,128)S(1)} %get-tuple-element.32), channel_id=1, source_target_pairs={{8,0},{16,8},{24,16},{32,24},{40,32},{48,40},{56,48},{64,56},{72,6... | collective-permute-start | bytes 1966088 | tf_op jit(solution)/shard_map/ppermute | solution.py:16
  71.5 13.1 %collective-permute-start.8 = (f32[2,4,128,128]{3,2,1,0:T(8,128)S(1)}, f32[2,4,128,128]{3,2,1,0:T(8,128)S(1)}, u32[]{:S(2)}, u32[]{:S(2)}) collective-permute-start(f32[2,4,128,128]{3,2,1,0:T(8,128)S(1)} %pad_maximum_fusion.2), channel_id=1, source_target_pairs={{0,7},{1,0},{2,1},{3,2},{4,3},{5,4},{6,5},{7,6},{8,15},{9,8},{10,9... | collective-permute-start | bytes 1572872 | tf_op jit(solution)/shard_map/ppermute | solution.py:22
  76.2 14.7 %collective-permute-start.9 = (f32[5,2,128,128]{3,2,1,0:T(8,128)S(1)}, f32[5,2,128,128]{3,2,1,0:T(8,128)S(1)}, u32[]{:S(2)}, u32[]{:S(2)}) collective-permute-start(f32[5,2,128,128]{3,2,1,0:T(8,128)S(1)} %get-tuple-element.29), channel_id=1, source_target_pairs={{0,8},{8,16},{16,24},{24,32},{32,40},{40,48},{48,56},{56,64},{64,7... | collective-permute-start | bytes 1966088 | tf_op jit(solution)/shard_map/ppermute | solution.py:15
  78.2 14.4 %collective-permute-start.10 = (f32[5,2,128,128]{3,2,1,0:T(8,128)S(1)}, f32[5,2,128,128]{3,2,1,0:T(8,128)S(1)}, u32[]{:S(2)}, u32[]{:S(2)}) collective-permute-start(f32[5,2,128,128]{3,2,1,0:T(8,128)S(1)} %get-tuple-element.30), channel_id=1, source_target_pairs={{8,0},{16,8},{24,16},{32,24},{40,32},{48,40},{56,48},{64,56},{72,6... | collective-permute-start | bytes 1966088 | tf_op jit(solution)/shard_map/ppermute | solution.py:16
  95.0 15.0 %collective-permute-start.11 = (f32[2,4,128,128]{3,2,1,0:T(8,128)S(1)}, f32[2,4,128,128]{3,2,1,0:T(8,128)S(1)}, u32[]{:S(2)}, u32[]{:S(2)}) collective-permute-start(f32[2,4,128,128]{3,2,1,0:T(8,128)S(1)} %pad_maximum_fusion.3), channel_id=1, source_target_pairs={{0,3},{1,4},{2,5},{3,6},{4,7},{5,0},{6,1},{7,2},{8,11},{9,12},{10,... | collective-permute-start | bytes 1572872 | tf_op jit(solution)/shard_map/ppermute | solution.py:22

commit v2 on v1

v2 whole, which is shorter than its diff:
```python
import functools

import jax
import jax.numpy as jnp
from jax import lax
from jax.experimental import pallas as pl
from jax.experimental.pallas import tpu as pltpu
from jax.sharding import PartitionSpec as P

STEPS = 5
TICKS = 4
TIME_STEP_SQ = 0.12
ROWS = 128
PAD = 8
LAG = 8
MESH = pl.DeviceIdType.MESH

FIRST_BOUNDS = (0, 32, 64, 96, 128)
BOUNDS = (
    (0, 32, 64, 96, 128),
    (0, 24, 56, 88, 128),
    (0, 16, 48, 88, 128),
    (0, 8, 48, 88, 128),
    (0, 8, 48, 88, 128),
)
CHUNKS = 4


def emitted(window, arrived):
    return ROWS if arrived == ROWS else max(0, arrived - STEPS * LAG)


class Place:
    def __init__(self, nz):
        s, i = lax.axis_index("space"), lax.axis_index("iter")
        self.nz = nz
        self.core = lax.rem(s, 2)
        self.z = lax.rem(lax.div(s, 2), nz)
        x_lo = lax.div(s, 2 * nz)
        self.y = lax.div(i, 2)
        self.x = 2 * lax.rem(i, 2) + x_lo
        self.s, self.i = s, i
        self.dir = 1 - 2 * self.core

    def at(self, dx, dy):
        x = lax.rem(self.x + dx + 8, 4)
        y = lax.rem(self.y + dy + 8, 4)
        return {
            "space": lax.rem(x, 2) * 2 * self.nz + self.z * 2 + self.core,
            "iter": y * 2 + lax.div(x, 2),
        }

    def hi(self, dx):
        return lax.div(lax.rem(self.x + dx + 8, 4), 2)

    def dy_back(self, h):
        return 0, h - 1

    def dy_home(self, h):
        c = self.core
        first = h * (1 - 2 * c) + (1 - h) * (1 - c)
        second = h * (1 - 2 * c) + (1 - h) * c
        return first, second

    def routes(self, dys):
        d = self.dir
        h = self.hi(0)
        first_to = self.at(d, dys(h)[0])
        h_in = self.hi(-d)
        first_from = self.at(-d, -dys(h_in)[0])
        second_to = self.at(d, dys(h_in)[1])
        second_from = self.at(-d, -dys(1 - h)[1])
        return first_to, first_from, second_to, second_from


def kernel(nz, start, prior, speed, kerr, out,
           v, path0, halo, relay, wk, raw, h_send, h_recv, a_send, a_recv, b_send, b_recv, l_sem):
    me = Place(nz)
    count = 4 * nz
    back = me.routes(me.dy_back)
    home = me.routes(me.dy_home)
    up = {"space": me.s + 1}
    down = {"space": me.s - 1}

    loads = [
        pltpu.make_async_copy(speed, raw.at[0], l_sem.at[0]),
        pltpu.make_async_copy(kerr, raw.at[1], l_sem.at[1]),
        pltpu.make_async_copy(start, v.at[0, 0:2, :, pl.ds(PAD, ROWS), :], l_sem.at[2]),
        pltpu.make_async_copy(prior, path0, l_sem.at[3]),
    ]
    for load in loads:
        load.start()

    barrier = pltpu.get_barrier_semaphore()
    for writer in (back[1], back[3], home[1], home[3]):
        pl.semaphore_signal(barrier, inc=1, device_id=writer, device_id_type=MESH)

    for near in (lax.rem(me.s + 1, count), lax.rem(me.s + count - 1, count)):
        pl.semaphore_signal(barrier, inc=1, device_id={"space": near}, device_id_type=MESH)

    zero = jnp.zeros((STEPS, 4, PAD, 128), jnp.float32)
    for t in range(TICKS):
        v[t, 1:6, :, 0:PAD, :] = zero
        v[t, 1:6, :, PAD + ROWS:, :] = zero

    @pl.when(me.s == 0)
    def _():
        @pl.loop(0, TICKS * STEPS)
        def _(k):
            halo[0, k] = jnp.zeros((2, ROWS, 128), jnp.float32)

    @pl.when(me.s == count - 1)
    def _():
        @pl.loop(0, TICKS * STEPS)
        def _(k):
            halo[1, k] = jnp.zeros((2, ROWS, 128), jnp.float32)

    pl.semaphore_wait(barrier, 6)

    def halo_copy(t, j, side):
        lo, hi = BOUNDS[t][j], BOUNDS[t][j + 1]
        planes = pl.ds(2, 2) if side == 0 else pl.ds(0, 2)
        if t == 0:
            src = prior.at[:, planes, pl.ds(lo, hi - lo), :]
        else:
            src = v.at[t - 1, 1:6, planes, pl.ds(PAD + lo, hi - lo), :]
        return pltpu.make_async_remote_copy(
            src_ref=src,
            dst_ref=halo.at[side, pl.ds(STEPS * t, STEPS), :, pl.ds(lo, hi - lo), :],
            send_sem=h_send.at[t, j, side],
            recv_sem=h_recv.at[t, j, side],
            device_id=up if side == 0 else down,
            device_id_type=MESH,
        )

    def send_halo(t, j):
        @pl.when(me.s < count - 1)
        def _():
            halo_copy(t, j, 0).start()

        @pl.when(me.s > 0)
        def _():
            halo_copy(t, j, 1).start()

    def wait_halo(t, j):
        @pl.when(me.s > 0)
        def _():
            halo_copy(t, j, 0).wait_recv()

        @pl.when(me.s < count - 1)
        def _():
            halo_copy(t, j, 1).wait_recv()

    def wait_halo_sent(t, j):
        @pl.when(me.s < count - 1)
        def _():
            halo_copy(t, j, 0).wait_send()

        @pl.when(me.s > 0)
        def _():
            halo_copy(t, j, 1).wait_send()

    def first_hop(t, j):
        lo, hi = BOUNDS[t][j], BOUNDS[t][j + 1]
        return pltpu.make_async_remote_copy(
            src_ref=v.at[t - 1, 5:7, :, pl.ds(PAD + lo, hi - lo), :],
            dst_ref=relay.at[t - 1, :, :, pl.ds(lo, hi - lo), :],
            send_sem=a_send.at[t - 1, j],
            recv_sem=a_recv.at[t - 1, j],
            device_id=(back if t < TICKS else home)[0],
            device_id_type=MESH,
        )

    def second_hop(t, j):
        lo, hi = BOUNDS[t][j], BOUNDS[t][j + 1]
        if t < TICKS:
            dst = v.at[t, 0:2, :, pl.ds(PAD + lo, hi - lo), :]
        else:
            dst = out.at[:, :, pl.ds(lo, hi - lo), :]
        return pltpu.make_async_remote_copy(
            src_ref=relay.at[t - 1, :, :, pl.ds(lo, hi - lo), :],
            dst_ref=dst,
            send_sem=b_send.at[t - 1, j],
            recv_sem=b_recv.at[t - 1, j],
            device_id=(back if t < TICKS else home)[2],
            device_id_type=MESH,
        )

    for j in range(CHUNKS):
        send_halo(0, j)

    loads[0].wait()
    loads[1].wait()

    @pl.loop(0, ROWS // 8)
    def _(k):
        rows = pl.ds(pl.multiple_of(k * 8, 8), 8)
        wk[0, :, rows, :] = raw[0, :, rows, :] * (TIME_STEP_SQ / 12.0)
        wk[1, :, rows, :] = raw[1, :, rows, :] * TIME_STEP_SQ

    loads[2].wait()
    loads[3].wait()

    lane = lax.broadcasted_iota(jnp.int32, (8, 128), 1)

    def step_block(t, n, r):
        mid = pl.ds(r + PAD, 8)
        rows = pl.ds(r, 8)
        tile = lambda z, off: v[t, n + 1, z, pl.ds(r + PAD + off, 8), :]
        u = [tile(z, 0) for z in range(4)]
        col = [halo[0, STEPS * t + n, 0, rows, :], halo[0, STEPS * t + n, 1, rows, :], *u,
               halo[1, STEPS * t + n, 0, rows, :], halo[1, STEPS * t + n, 1, rows, :]]
        for z in range(4):
            c = u[z]
            above, below = v[t, n + 1, z, pl.ds(r, 8), :], v[t, n + 1, z, pl.ds(r + 2 * PAD, 8), :]
            band = jnp.concatenate([above, c, below], axis=0)
            s1 = band[7:15] + band[9:17]
            s2 = band[6:14] + band[10:18]
            s1 += col[z + 1] + col[z + 3]
            s2 += col[z] + col[z + 4]
            s1 += jnp.where(lane < 1, 0.0, pltpu.roll(c, 1, 1)) + jnp.where(lane > 126, 0.0, pltpu.roll(c, 127, 1))
            s2 += jnp.where(lane < 2, 0.0, pltpu.roll(c, 2, 1)) + jnp.where(lane > 125, 0.0, pltpu.roll(c, 126, 1))
            laplace = 16.0 * s1 - s2 - 90.0 * c
            g = path0[n, z, rows, :] if t == 0 else v[t - 1, n + 1, z, mid, :]
            kg = wk[1, z, rows, :] * (g * g)
            v[t, n + 2, z, mid, :] = (
                (2.0 * c - v[t, n, z, mid, :]) + wk[0, z, rows, :] * laplace + kg * (2.0 * g - 3.0 * c)
            )

    def step_rows(t, n, lo, hi):
        if hi <= lo:
            return

        @pl.loop(0, (hi - lo) // 8)
        def _(k):
            step_block(t, n, pl.multiple_of(lo + k * 8, 8))

    for t in range(TICKS):
        bounds = BOUNDS[t]
        sent = 0
        for j in range(CHUNKS):
            if t > 0:
                first_hop(t, j).wait_recv()
                second_hop(t, j).start()
            if t > 0:
                second_hop(t, j).wait_recv()
            wait_halo(t, j)
            lo, hi = bounds[j], bounds[j + 1]
            for n in range(STEPS):
                lag = LAG * (n + 1)
                step_rows(t, n, max(0, lo - lag), ROWS if hi == ROWS else max(0, hi - lag))
            ready = emitted(t, hi)
            while sent < CHUNKS and BOUNDS[t + 1][sent + 1] <= ready:
                first_hop(t + 1, sent).start()
                if t + 1 < TICKS:
                    send_halo(t + 1, sent)
                sent += 1
    for j in range(CHUNKS):
        first_hop(TICKS, j).wait_recv()
        second_hop(TICKS, j).start()
    for j in range(CHUNKS):
        second_hop(TICKS, j).wait_recv()
    for t in range(TICKS):
        for j in range(CHUNKS):
            wait_halo_sent(t, j)
            first_hop(t + 1, j).wait_send()
            second_hop(t + 1, j).wait_send()


def per_device(nz, start_state, prior_path, wave_speed, kerr_coeff):
    any_space = pl.BlockSpec(memory_space=pl.ANY)
    out = pl.pallas_call(
        functools.partial(kernel, nz),
        out_shape=jax.ShapeDtypeStruct((2, 4, ROWS, 128), jnp.float32),
        in_specs=[any_space] * 4,
        out_specs=any_space,
        scratch_shapes=[
            pltpu.VMEM((TICKS, 7, 4, ROWS + 2 * PAD, 128), jnp.float32),
            pltpu.VMEM((STEPS, 4, ROWS, 128), jnp.float32),
            pltpu.VMEM((2, TICKS * STEPS, 2, ROWS, 128), jnp.float32),
            pltpu.VMEM((TICKS, 2, 4, ROWS, 128), jnp.float32),
            pltpu.VMEM((2, 4, ROWS, 128), jnp.float32),
            pltpu.VMEM((2, 4, ROWS, 128), jnp.float32),
            pltpu.SemaphoreType.DMA((TICKS, CHUNKS, 2)),
            pltpu.SemaphoreType.DMA((TICKS, CHUNKS, 2)),
            pltpu.SemaphoreType.DMA((TICKS, CHUNKS)),
            pltpu.SemaphoreType.DMA((TICKS, CHUNKS)),
            pltpu.SemaphoreType.DMA((TICKS, CHUNKS)),
            pltpu.SemaphoreType.DMA((TICKS, CHUNKS)),
            pltpu.SemaphoreType.DMA((4,)),
        ],
        compiler_params=pltpu.CompilerParams(
            collective_id=0, has_side_effects=True, vmem_limit_bytes=40 << 20
        ),
        name="relaxation",
    )(start_state[0], prior_path[0], wave_speed, kerr_coeff)
    return out[None]


def solution(mesh):
    nz = mesh.shape["space"] // 4
    return jax.shard_map(
        functools.partial(per_device, nz),
        mesh=mesh,
        in_specs=(
            P("iter", None, "space", None, None),
            P("iter", None, "space", None, None),
            P("space", None, None),
            P("space", None, None),
        ),
        out_specs=P("iter", None, "space", None, None),
        check_vma=False,
    )
```

time: 111 us -> 146 us (1.32)
  the two profiles are of different devices: /device:TPU:2 before, /device:TPU:8 now
where the time goes in v2:
time: 146 us
  Pallas kernels  141 us (97%)
  local copies, waits for them, and re-layouts  5.05 us (3%)
    pallas_call x1, Pallas kernels, per_device(): pl.pallas_call(functools.partial(kernel, nz), out_shape=jax.ShapeDtypeStr...  141 us
    unnamed x9, local copies, waits for them, and re-layouts  5.05 us

profile of v2, /device:TPU:8, one launch (start us, length us, event | category | flops | bytes accessed | tf_op | source)
XLA Modules:
  0.0 145.8 jit_solution(3568298028823438667)
XLA Ops:
  0.0 0.0 copy-start
  0.0 1.3 copy-done
  1.3 0.0 copy-start.1
  1.3 1.0 copy-done.1
  2.4 0.0 copy-start.2
  2.4 0.9 copy-done.2
  3.3 0.0 copy-start.3
  3.3 0.9 copy-done.3
  4.3 140.7 %relaxation.1 = f32[2,4,128,128]{3,2,1,0:T(8,128)S(1)} custom-call(f32[2,4,128,128]{3,2,1,0:T(8,128)S(1)} %bitcast.5, f32[5,4,128,128]{3,2,1,0:T(8,128)S(1)} %bitcast.4, f32[4,128,128]{2,1,0:T(8,128)S(1)} %copy-done.2, f32[4,128,128]{2,1,0:T(8,128)S(1)} %copy-done.3), custom_call_target="tpu_custom_call" | custom-call | tf_op jit(solution)/shard_map/relaxation/pallas_call | solution.py:272
  145.0 0.8 copy.6
Async XLA Ops:
  0.0 1.3 copy-start
  1.3 1.0 copy-start.1
  2.4 0.9 copy-start.2
  3.3 0.9 copy-start.3

commit v3 on v2

v3 whole, which is shorter than its diff:
```python
import functools

import jax
import jax.numpy as jnp
from jax import lax
from jax.experimental import pallas as pl
from jax.experimental.pallas import tpu as pltpu
from jax.sharding import PartitionSpec as P

STEPS = 5
TICKS = 4
TIME_STEP_SQ = 0.12
ROWS = 128
PAD = 8
LAG = 8
MESH = pl.DeviceIdType.MESH

FIRST_BOUNDS = (0, 32, 64, 96, 128)
BOUNDS = (
    (0, 32, 64, 96, 128),
    (0, 24, 56, 88, 128),
    (0, 16, 48, 88, 128),
    (0, 8, 48, 88, 128),
    (0, 8, 48, 88, 128),
)
CHUNKS = 4


def emitted(window, arrived):
    return ROWS if arrived == ROWS else max(0, arrived - STEPS * LAG)


class Place:
    def __init__(self, nz):
        s, i = lax.axis_index("space"), lax.axis_index("iter")
        self.nz = nz
        self.core = lax.rem(s, 2)
        self.z = lax.rem(lax.div(s, 2), nz)
        x_lo = lax.div(s, 2 * nz)
        self.y = lax.div(i, 2)
        self.x = 2 * lax.rem(i, 2) + x_lo
        self.s, self.i = s, i
        self.h = lax.rem(i, 2)

    def at(self, dx, dy):
        x = lax.rem(self.x + dx + 8, 4)
        y = lax.rem(self.y + dy + 8, 4)
        return {
            "space": lax.rem(x, 2) * 2 * self.nz + self.z * 2 + self.core,
            "iter": y * 2 + lax.div(x, 2),
        }

    def back(self):
        return self.at(2, self.h - 1), self.at(2, self.h)

    def home(self):
        return self.at(2, 1 + self.h), self.at(2, self.h - 2)


def kernel(nz, start, prior, speed, kerr, out,
           v, path0, halo, wk, raw, h_send, h_recv, s_send, s_recv, l_sem):
    me = Place(nz)
    count = 4 * nz
    back = me.back()
    home = me.home()
    up = {"space": me.s + 1}
    down = {"space": me.s - 1}

    loads = [
        pltpu.make_async_copy(speed, raw.at[0], l_sem.at[0]),
        pltpu.make_async_copy(kerr, raw.at[1], l_sem.at[1]),
        pltpu.make_async_copy(start, v.at[0, 0:2, :, pl.ds(PAD, ROWS), :], l_sem.at[2]),
        pltpu.make_async_copy(prior, path0, l_sem.at[3]),
    ]
    for load in loads:
        load.start()

    barrier = pltpu.get_barrier_semaphore()
    for writer in (back[1], home[1]):
        pl.semaphore_signal(barrier, inc=1, device_id=writer, device_id_type=MESH)

    for near in (lax.rem(me.s + 1, count), lax.rem(me.s + count - 1, count)):
        pl.semaphore_signal(barrier, inc=1, device_id={"space": near}, device_id_type=MESH)

    zero = jnp.zeros((STEPS, 4, PAD, 128), jnp.float32)
    for t in range(TICKS):
        v[t, 1:6, :, 0:PAD, :] = zero
        v[t, 1:6, :, PAD + ROWS:, :] = zero

    @pl.when(me.s == 0)
    def _():
        @pl.loop(0, TICKS * STEPS)
        def _(k):
            halo[0, k] = jnp.zeros((2, ROWS, 128), jnp.float32)

    @pl.when(me.s == count - 1)
    def _():
        @pl.loop(0, TICKS * STEPS)
        def _(k):
            halo[1, k] = jnp.zeros((2, ROWS, 128), jnp.float32)

    pl.semaphore_wait(barrier, 4)

    def halo_copy(t, j, side):
        lo, hi = BOUNDS[t][j], BOUNDS[t][j + 1]
        planes = pl.ds(2, 2) if side == 0 else pl.ds(0, 2)
        if t == 0:
            src = prior.at[:, planes, pl.ds(lo, hi - lo), :]
        else:
            src = v.at[t - 1, 1:6, planes, pl.ds(PAD + lo, hi - lo), :]
        return pltpu.make_async_remote_copy(
            src_ref=src,
            dst_ref=halo.at[side, pl.ds(STEPS * t, STEPS), :, pl.ds(lo, hi - lo), :],
            send_sem=h_send.at[t, j, side],
            recv_sem=h_recv.at[t, j, side],
            device_id=up if side == 0 else down,
            device_id_type=MESH,
        )

    def send_halo(t, j):
        @pl.when(me.s < count - 1)
        def _():
            halo_copy(t, j, 0).start()

        @pl.when(me.s > 0)
        def _():
            halo_copy(t, j, 1).start()

    def wait_halo(t, j):
        @pl.when(me.s > 0)
        def _():
            halo_copy(t, j, 0).wait_recv()

        @pl.when(me.s < count - 1)
        def _():
            halo_copy(t, j, 1).wait_recv()

    def wait_halo_sent(t, j):
        @pl.when(me.s < count - 1)
        def _():
            halo_copy(t, j, 0).wait_send()

        @pl.when(me.s > 0)
        def _():
            halo_copy(t, j, 1).wait_send()

    def state_copy(t, j):
        lo, hi = BOUNDS[t][j], BOUNDS[t][j + 1]
        if t < TICKS:
            dst = v.at[t, 0:2, :, pl.ds(PAD + lo, hi - lo), :]
        else:
            dst = out.at[:, :, pl.ds(lo, hi - lo), :]
        return pltpu.make_async_remote_copy(
            src_ref=v.at[t - 1, 5:7, :, pl.ds(PAD + lo, hi - lo), :],
            dst_ref=dst,
            send_sem=s_send.at[t - 1, j],
            recv_sem=s_recv.at[t - 1, j],
            device_id=(back if t < TICKS else home)[0],
            device_id_type=MESH,
        )

    for j in range(CHUNKS):
        send_halo(0, j)

    loads[0].wait()
    loads[1].wait()

    @pl.loop(0, ROWS // 8)
    def _(k):
        rows = pl.ds(pl.multiple_of(k * 8, 8), 8)
        scaled = raw[0, :, rows, :] * (TIME_STEP_SQ / 12.0)
        wk[0, :, rows, :] = scaled
        wk[1, :, rows, :] = raw[1, :, rows, :] * (3.0 * TIME_STEP_SQ)
        wk[2, :, rows, :] = 2.0 - 90.0 * scaled

    loads[2].wait()
    loads[3].wait()

    def step_block(t, n, r, size):
        mid = pl.ds(r + PAD, size)
        rows = pl.ds(r, size)
        lane = lax.broadcasted_iota(jnp.int32, (size, 128), 1)
        k = STEPS * t + n
        col = [halo[0, k, 0, rows, :], halo[0, k, 1, rows, :],
               *[v[t, n + 1, z, mid, :] for z in range(4)],
               halo[1, k, 0, rows, :], halo[1, k, 1, rows, :]]
        for z in range(4):
            c = col[z + 2]

            def shifted(off):
                return v[t, n + 1, z, pl.ds(r + PAD + off, size), :]

            def turned(off):
                inside = lane >= off if off > 0 else lane < 128 + off
                return jnp.where(inside, pltpu.roll(c, off % 128, 1), 0.0)

            s1 = (shifted(-1) + shifted(1)) + (col[z + 1] + col[z + 3]) + (turned(-1) + turned(1))
            s2 = (shifted(-2) + shifted(2)) + (col[z] + col[z + 4]) + (turned(-2) + turned(2))
            g = path0[n, z, rows, :] if t == 0 else v[t - 1, n + 1, z, mid, :]
            v[t, n + 2, z, mid, :] = (
                (wk[2, z, rows, :] * c - v[t, n, z, mid, :])
                + wk[0, z, rows, :] * (16.0 * s1 - s2)
                + (wk[1, z, rows, :] * (g * g)) * ((2.0 / 3.0) * g - c)
            )

    def step_rows(t, n, lo, hi):
        if hi <= lo:
            return
        size = 16
        for r in range(lo, hi, size):
            step_block(t, n, r, min(size, hi - r))

    for t in range(TICKS):
        bounds = BOUNDS[t]
        sent = 0
        for j in range(CHUNKS):
            if t > 0:
                state_copy(t, j).wait_recv()
            wait_halo(t, j)
            lo, hi = bounds[j], bounds[j + 1]
            for n in range(STEPS):
                lag = LAG * (n + 1)
                step_rows(t, n, max(0, lo - lag), ROWS if hi == ROWS else max(0, hi - lag))
            ready = emitted(t, hi)
            while sent < CHUNKS and BOUNDS[t + 1][sent + 1] <= ready:
                state_copy(t + 1, sent).start()
                if t + 1 < TICKS:
                    send_halo(t + 1, sent)
                sent += 1
    for j in range(CHUNKS):
        state_copy(TICKS, j).wait_recv()
    for t in range(TICKS):
        for j in range(CHUNKS):
            wait_halo_sent(t, j)
            state_copy(t + 1, j).wait_send()


def per_device(nz, start_state, prior_path, wave_speed, kerr_coeff):
    any_space = pl.BlockSpec(memory_space=pl.ANY)
    out = pl.pallas_call(
        functools.partial(kernel, nz),
        out_shape=jax.ShapeDtypeStruct((2, 4, ROWS, 128), jnp.float32),
        in_specs=[any_space] * 4,
        out_specs=any_space,
        scratch_shapes=[
            pltpu.VMEM((TICKS, 7, 4, ROWS + 2 * PAD, 128), jnp.float32),
            pltpu.VMEM((STEPS, 4, ROWS, 128), jnp.float32),
            pltpu.VMEM((2, TICKS * STEPS, 2, ROWS, 128), jnp.float32),
            pltpu.VMEM((3, 4, ROWS, 128), jnp.float32),
            pltpu.VMEM((2, 4, ROWS, 128), jnp.float32),
            pltpu.SemaphoreType.DMA((TICKS, CHUNKS, 2)),
            pltpu.SemaphoreType.DMA((TICKS, CHUNKS, 2)),
            pltpu.SemaphoreType.DMA((TICKS, CHUNKS)),
            pltpu.SemaphoreType.DMA((TICKS, CHUNKS)),
            pltpu.SemaphoreType.DMA((4,)),
        ],
        compiler_params=pltpu.CompilerParams(
            collective_id=0, has_side_effects=True, vmem_limit_bytes=62 << 20
        ),
        name="relaxation",
    )(start_state[0], prior_path[0], wave_speed, kerr_coeff)
    return out[None]


def solution(mesh):
    nz = mesh.shape["space"] // 4
    return jax.shard_map(
        functools.partial(per_device, nz),
        mesh=mesh,
        in_specs=(
            P("iter", None, "space", None, None),
            P("iter", None, "space", None, None),
            P("space", None, None),
            P("space", None, None),
        ),
        out_specs=P("iter", None, "space", None, None),
        check_vma=False,
    )
```

time: 146 us -> 94.4 us (0.65)
  the two profiles are of different devices: /device:TPU:8 before, /device:TPU:1 now
where the time goes in v3:
time: 94.4 us; the launch traced here: 94.2 us
  Pallas kernels  92.3 us (98%)
  local copies, waits for them, and re-layouts  1.87 us (2%)
    pallas_call x1, Pallas kernels, per_device(): pl.pallas_call(functools.partial(kernel, nz), out_shape=jax.ShapeDtypeStr...  92.3 us

profile of v3, /device:TPU:1, one launch (start us, length us, event | category | flops | bytes accessed | tf_op | source)
XLA Modules:
  0.0 94.2 jit_solution(12969113611712566475)
XLA Ops:
  0.0 92.3 %relaxation.1 = f32[2,4,128,128]{3,2,1,0:T(8,128)} custom-call(f32[2,4,128,128]{3,2,1,0:T(8,128)} %bitcast.5, f32[5,4,128,128]{3,2,1,0:T(8,128)} %bitcast.4, f32[4,128,128]{2,1,0:T(8,128)} %speed.1, f32[4,128,128]{2,1,0:T(8,128)} %kerr.1), custom_call_target="tpu_custom_call" | custom-call | tf_op jit(solution)/shard_map/relaxation/pallas_call | solution.py:240
  92.3 1.9 %copy.6 = f32[1,2,4,128,128]{4,3,2,1,0:T(8,128)} copy(f32[1,2,4,128,128]{4,3,2,1,0:T(8,128)} %bitcast.3) | data formatting | bytes 1048576

commit v4 on v3

--- a/solution.py
+++ b/solution.py
@@ -12,22 +12,22 @@
 TIME_STEP_SQ = 0.12
 ROWS = 128
 PAD = 8
-LAG = 8
+LAG = 2
 MESH = pl.DeviceIdType.MESH
 
-FIRST_BOUNDS = (0, 32, 64, 96, 128)
 BOUNDS = (
     (0, 32, 64, 96, 128),
-    (0, 24, 56, 88, 128),
-    (0, 16, 48, 88, 128),
-    (0, 8, 48, 88, 128),
-    (0, 8, 48, 88, 128),
+    (0, 16, 48, 80, 128),
+    (0, 32, 64, 96, 128),
+    (0, 16, 48, 80, 128),
+    (0, 32, 64, 96, 128),
 )
 CHUNKS = 4
+FORWARD_AFTER = 2
 
 
 def emitted(window, arrived):
-    return ROWS if arrived == ROWS else max(0, arrived - STEPS * LAG)
+    return ROWS if arrived == ROWS else max(0, arrived - STEPS * LAG) // 8 * 8
 
 
 class Place:
@@ -58,13 +58,20 @@
 
 
 def kernel(nz, start, prior, speed, kerr, out,
-           v, path0, halo, wk, raw, h_send, h_recv, s_send, s_recv, l_sem):
+           v, path0, halo, passing, wk, raw, h_send, h_recv, s_send, s_recv, p_send, p_recv, l_sem):
     me = Place(nz)
     count = 4 * nz
     back = me.back()
     home = me.home()
     up = {"space": me.s + 1}
     down = {"space": me.s - 1}
+    half = count // 2
+    last = nz - 1
+    ends = (half - 1, half)
+    passers = (
+        [half + 2 * z for z in (last, 1, last - 1)],
+        [1 + 2 * z for z in (0, 1, last - 1)],
+    )
 
     loads = [
         pltpu.make_async_copy(speed, raw.at[0], l_sem.at[0]),
@@ -82,6 +89,16 @@
     for near in (lax.rem(me.s + 1, count), lax.rem(me.s + count - 1, count)):
         pl.semaphore_signal(barrier, inc=1, device_id={"space": near}, device_id_type=MESH)
 
+    for side in range(2):
+        for passer in passers[side]:
+            @pl.when(me.s == passer)
+            def _():
+                pl.semaphore_signal(barrier, inc=1, device_id={"space": ends[side]}, device_id_type=MESH)
+
+            @pl.when(me.s == ends[1 - side])
+            def _():
+                pl.semaphore_signal(barrier, inc=1, device_id={"space": passer}, device_id_type=MESH)
+
     zero = jnp.zeros((STEPS, 4, PAD, 128), jnp.float32)
     for t in range(TICKS):
         v[t, 1:6, :, 0:PAD, :] = zero
@@ -99,7 +116,12 @@
         def _(k):
             halo[1, k] = jnp.zeros((2, ROWS, 128), jnp.float32)
 
-    pl.semaphore_wait(barrier, 4)
+    peers = jnp.int32(4)
+    for side in range(2):
+        peers += 3 * (me.s == ends[side]).astype(jnp.int32)
+        for passer in passers[side]:
+            peers += (me.s == passer).astype(jnp.int32)
+    pl.semaphore_wait(barrier, peers)
 
     def halo_copy(t, j, side):
         lo, hi = BOUNDS[t][j], BOUNDS[t][j + 1]
@@ -117,14 +139,54 @@
             device_id_type=MESH,
         )
 
+    def pass_in(t, j, side):
+        lo, hi = BOUNDS[t][j], BOUNDS[t][j + 1]
+        return pltpu.make_async_remote_copy(
+            src_ref=v.at[t - 1, 1:6, pl.ds(2 - 2 * side, 2), pl.ds(PAD + lo, hi - lo), :],
+            dst_ref=passing.at[t - 1, :, :, pl.ds(lo, hi - lo), :],
+            send_sem=h_send.at[t, j, side],
+            recv_sem=p_recv.at[t - 1, j],
+            device_id={"space": passers[side][j - 1]},
+            device_id_type=MESH,
+        )
+
+    def pass_out(t, j, side):
+        lo, hi = BOUNDS[t][j], BOUNDS[t][j + 1]
+        return pltpu.make_async_remote_copy(
+            src_ref=passing.at[t - 1, :, :, pl.ds(lo, hi - lo), :],
+            dst_ref=halo.at[side, pl.ds(STEPS * t, STEPS), :, pl.ds(lo, hi - lo), :],
+            send_sem=p_send.at[t - 1, j],
+            recv_sem=h_recv.at[t, j, side],
+            device_id={"space": ends[1 - side]},
+            device_id_type=MESH,
+        )
+
+    def forward(t, j):
+        for side in range(2):
+            @pl.when(me.s == passers[side][j - 1])
+            def _():
+                pass_in(t, j, side).wait_recv()
+                pass_out(t, j, side).start()
+
+    def wait_forwarded(t, j):
+        for side in range(2):
+            @pl.when(me.s == passers[side][j - 1])
+            def _():
+                pass_out(t, j, side).wait_send()
+
     def send_halo(t, j):
-        @pl.when(me.s < count - 1)
-        def _():
-            halo_copy(t, j, 0).start()
-
-        @pl.when(me.s > 0)
-        def _():
-            halo_copy(t, j, 1).start()
+        roundabout = t > 0 and j > 0
+        for side, near in ((0, me.s < count - 1), (1, me.s > 0)):
+            if roundabout:
+                near = near & (me.s != ends[side])
+
+                @pl.when(me.s == ends[side])
+                def _():
+                    pass_in(t, j, side).start()
+
+            @pl.when(near)
+            def _():
+                halo_copy(t, j, side).start()
 
     def wait_halo(t, j):
         @pl.when(me.s > 0)
@@ -210,10 +272,14 @@
         for r in range(lo, hi, size):
             step_block(t, n, r, min(size, hi - r))
 
+    forwards = []
     for t in range(TICKS):
         bounds = BOUNDS[t]
         sent = 0
         for j in range(CHUNKS):
+            event = CHUNKS * t + j
+            while forwards and forwards[0][0] + FORWARD_AFTER <= event:
+                forward(*forwards.pop(0)[1:])
             if t > 0:
                 state_copy(t, j).wait_recv()
             wait_halo(t, j)
@@ -226,12 +292,16 @@
                 state_copy(t + 1, sent).start()
                 if t + 1 < TICKS:
                     send_halo(t + 1, sent)
+                    if sent:
+                        forwards.append((event, t + 1, sent))
                 sent += 1
     for j in range(CHUNKS):
         state_copy(TICKS, j).wait_recv()
     for t in range(TICKS):
         for j in range(CHUNKS):
             wait_halo_sent(t, j)
+            if t and j:
+                wait_forwarded(t, j)
             state_copy(t + 1, j).wait_send()
 
 
@@ -246,12 +316,15 @@
             pltpu.VMEM((TICKS, 7, 4, ROWS + 2 * PAD, 128), jnp.float32),
             pltpu.VMEM((STEPS, 4, ROWS, 128), jnp.float32),
             pltpu.VMEM((2, TICKS * STEPS, 2, ROWS, 128), jnp.float32),
+            pltpu.VMEM((TICKS - 1, STEPS, 2, ROWS, 128), jnp.float32),
             pltpu.VMEM((3, 4, ROWS, 128), jnp.float32),
             pltpu.VMEM((2, 4, ROWS, 128), jnp.float32),
             pltpu.SemaphoreType.DMA((TICKS, CHUNKS, 2)),
             pltpu.SemaphoreType.DMA((TICKS, CHUNKS, 2)),
             pltpu.SemaphoreType.DMA((TICKS, CHUNKS)),
             pltpu.SemaphoreType.DMA((TICKS, CHUNKS)),
+            pltpu.SemaphoreType.DMA((TICKS - 1, CHUNKS)),
+            pltpu.SemaphoreType.DMA((TICKS - 1, CHUNKS)),
             pltpu.SemaphoreType.DMA((4,)),
         ],
         compiler_params=pltpu.CompilerParams(

time: 94.4 us -> 78.9 us (0.84)
  Pallas kernels: 92.3 us -> 76.9 us
    pallas_call x1, Pallas kernels: 92.3 us -> 76.9 us  [per_device(): pl.pallas_call(functools.partial(kernel, nz), out_shape=jax.ShapeDtypeStr...]
where the time goes in v4:
time: 78.9 us; the launch traced here: 78.7 us
  Pallas kernels  76.9 us (97%)
  local copies, waits for them, and re-layouts  1.87 us (2%)
    pallas_call x1, Pallas kernels, per_device(): pl.pallas_call(functools.partial(kernel, nz), out_shape=jax.ShapeDtypeStr...  76.9 us
    unnamed x1, local copies, waits for them, and re-layouts  1.87 us

profile of v4, /device:TPU:1, one launch (start us, length us, event | category | flops | bytes accessed | tf_op | source)
XLA Modules:
  0.0 78.7 jit_solution(16019001567772988518)
XLA Ops:
  0.0 76.9 %relaxation.1 = f32[2,4,128,128]{3,2,1,0:T(8,128)} custom-call(f32[2,4,128,128]{3,2,1,0:T(8,128)} %bitcast.5, f32[5,4,128,128]{3,2,1,0:T(8,128)} %bitcast.4, f32[4,128,128]{2,1,0:T(8,128)} %speed.1, f32[4,128,128]{2,1,0:T(8,128)} %kerr.1), custom_call_target="tpu_custom_call" | custom-call | tf_op jit(solution)/shard_map/relaxation/pallas_call | solution.py:310
  76.9 1.9 %copy.6 = f32[1,2,4,128,128]{4,3,2,1,0:T(8,128)} copy(f32[1,2,4,128,128]{4,3,2,1,0:T(8,128)} %bitcast.3) | data formatting | bytes 1048576

commit v5 on v4

--- a/solution.py
+++ b/solution.py
@@ -15,15 +15,9 @@
 LAG = 2
 MESH = pl.DeviceIdType.MESH
 
-BOUNDS = (
-    (0, 32, 64, 96, 128),
-    (0, 16, 48, 80, 128),
-    (0, 32, 64, 96, 128),
-    (0, 16, 48, 80, 128),
-    (0, 32, 64, 96, 128),
-)
-CHUNKS = 4
-FORWARD_AFTER = 2
+CHUNKS = 8
+BOUNDS = (tuple(range(0, ROWS + 1, ROWS // CHUNKS)),) * (TICKS + 1)
+FORWARD_AFTER = 3
 
 
 def emitted(window, arrived):
@@ -57,7 +51,7 @@
         return self.at(2, 1 + self.h), self.at(2, self.h - 2)
 
 
-def kernel(nz, start, prior, speed, kerr, out,
+def kernel(nz, start, prior, speed, kerr, out_prev, out_cur,
            v, path0, halo, passing, wk, raw, h_send, h_recv, s_send, s_recv, p_send, p_recv, l_sem):
     me = Place(nz)
     count = 4 * nz
@@ -69,8 +63,8 @@
     last = nz - 1
     ends = (half - 1, half)
     passers = (
-        [half + 2 * z for z in (last, 1, last - 1)],
-        [1 + 2 * z for z in (0, 1, last - 1)],
+        [half + 2 * z for z in (last, 1, last - 1, 2, last - 2, 3, last - 3)],
+        [1 + 2 * z for z in (0, 1, last - 1, 2, last - 2, 3, last - 3)],
     )
 
     loads = [
@@ -118,7 +112,7 @@
 
     peers = jnp.int32(4)
     for side in range(2):
-        peers += 3 * (me.s == ends[side]).astype(jnp.int32)
+        peers += len(passers[side]) * (me.s == ends[side]).astype(jnp.int32)
         for passer in passers[side]:
             peers += (me.s == passer).astype(jnp.int32)
     pl.semaphore_wait(barrier, peers)
@@ -139,23 +133,33 @@
             device_id_type=MESH,
         )
 
+    def passer_of(t, j, side):
+        if t == 0:
+            return passers[side][0] if j % 2 else None
+        return passers[side][(j - 1) % len(passers[side])] if j else None
+
     def pass_in(t, j, side):
         lo, hi = BOUNDS[t][j], BOUNDS[t][j + 1]
-        return pltpu.make_async_remote_copy(
-            src_ref=v.at[t - 1, 1:6, pl.ds(2 - 2 * side, 2), pl.ds(PAD + lo, hi - lo), :],
-            dst_ref=passing.at[t - 1, :, :, pl.ds(lo, hi - lo), :],
+        planes = pl.ds(2 - 2 * side, 2)
+        if t == 0:
+            src = prior.at[:, planes, pl.ds(lo, hi - lo), :]
+        else:
+            src = v.at[t - 1, 1:6, planes, pl.ds(PAD + lo, hi - lo), :]
+        return pltpu.make_async_remote_copy(
+            src_ref=src,
+            dst_ref=passing.at[t, :, :, pl.ds(lo, hi - lo), :],
             send_sem=h_send.at[t, j, side],
-            recv_sem=p_recv.at[t - 1, j],
-            device_id={"space": passers[side][j - 1]},
+            recv_sem=p_recv.at[t, j],
+            device_id={"space": passer_of(t, j, side)},
             device_id_type=MESH,
         )
 
     def pass_out(t, j, side):
         lo, hi = BOUNDS[t][j], BOUNDS[t][j + 1]
         return pltpu.make_async_remote_copy(
-            src_ref=passing.at[t - 1, :, :, pl.ds(lo, hi - lo), :],
+            src_ref=passing.at[t, :, :, pl.ds(lo, hi - lo), :],
             dst_ref=halo.at[side, pl.ds(STEPS * t, STEPS), :, pl.ds(lo, hi - lo), :],
-            send_sem=p_send.at[t - 1, j],
+            send_sem=p_send.at[t, j],
             recv_sem=h_recv.at[t, j, side],
             device_id={"space": ends[1 - side]},
             device_id_type=MESH,
@@ -163,19 +167,19 @@
 
     def forward(t, j):
         for side in range(2):
-            @pl.when(me.s == passers[side][j - 1])
+            @pl.when(me.s == passer_of(t, j, side))
             def _():
                 pass_in(t, j, side).wait_recv()
                 pass_out(t, j, side).start()
 
     def wait_forwarded(t, j):
         for side in range(2):
-            @pl.when(me.s == passers[side][j - 1])
+            @pl.when(me.s == passer_of(t, j, side))
             def _():
                 pass_out(t, j, side).wait_send()
 
     def send_halo(t, j):
-        roundabout = t > 0 and j > 0
+        roundabout = passer_of(t, j, 0) is not None
         for side, near in ((0, me.s < count - 1), (1, me.s > 0)):
             if roundabout:
                 near = near & (me.s != ends[side])
@@ -207,17 +211,25 @@
             halo_copy(t, j, 1).wait_send()
 
     def state_copy(t, j):
-        lo, hi = BOUNDS[t][j], BOUNDS[t][j + 1]
-        if t < TICKS:
-            dst = v.at[t, 0:2, :, pl.ds(PAD + lo, hi - lo), :]
-        else:
-            dst = out.at[:, :, pl.ds(lo, hi - lo), :]
-        return pltpu.make_async_remote_copy(
-            src_ref=v.at[t - 1, 5:7, :, pl.ds(PAD + lo, hi - lo), :],
-            dst_ref=dst,
+        rows = pl.ds(PAD + BOUNDS[t][j], BOUNDS[t][j + 1] - BOUNDS[t][j])
+        return pltpu.make_async_remote_copy(
+            src_ref=v.at[t - 1, 5:7, :, rows, :],
+            dst_ref=v.at[t, 0:2, :, rows, :],
             send_sem=s_send.at[t - 1, j],
             recv_sem=s_recv.at[t - 1, j],
-            device_id=(back if t < TICKS else home)[0],
+            device_id=back[0],
+            device_id_type=MESH,
+        )
+
+    def home_copy(j, level):
+        lo, hi = BOUNDS[TICKS][j], BOUNDS[TICKS][j + 1]
+        out = (out_prev, out_cur)[level]
+        return pltpu.make_async_remote_copy(
+            src_ref=v.at[TICKS - 1, 5 + level, :, pl.ds(PAD + lo, hi - lo), :],
+            dst_ref=out.at[:, pl.ds(lo, hi - lo), :],
+            send_sem=s_send.at[TICKS - 1 + level, j],
+            recv_sem=s_recv.at[TICKS - 1 + level, j],
+            device_id=home[0],
             device_id_type=MESH,
         )
 
@@ -272,14 +284,16 @@
         for r in range(lo, hi, size):
             step_block(t, n, r, min(size, hi - r))
 
-    forwards = []
+    forwards = [(j - FORWARD_AFTER, 0, j) for j in range(1, CHUNKS, 2)]
     for t in range(TICKS):
         bounds = BOUNDS[t]
         sent = 0
         for j in range(CHUNKS):
             event = CHUNKS * t + j
-            while forwards and forwards[0][0] + FORWARD_AFTER <= event:
-                forward(*forwards.pop(0)[1:])
+            due = [f for f in forwards if f[0] + FORWARD_AFTER <= event]
+            forwards = [f for f in forwards if f not in due]
+            for f in due:
+                forward(*f[1:])
             if t > 0:
                 state_copy(t, j).wait_recv()
             wait_halo(t, j)
@@ -289,42 +303,51 @@
                 step_rows(t, n, max(0, lo - lag), ROWS if hi == ROWS else max(0, hi - lag))
             ready = emitted(t, hi)
             while sent < CHUNKS and BOUNDS[t + 1][sent + 1] <= ready:
-                state_copy(t + 1, sent).start()
-                if t + 1 < TICKS:
+                if t + 1 == TICKS:
+                    home_copy(sent, 0).start()
+                    home_copy(sent, 1).start()
+                else:
+                    state_copy(t + 1, sent).start()
                     send_halo(t + 1, sent)
                     if sent:
                         forwards.append((event, t + 1, sent))
                 sent += 1
     for j in range(CHUNKS):
-        state_copy(TICKS, j).wait_recv()
+        home_copy(j, 0).wait_recv()
+        home_copy(j, 1).wait_recv()
     for t in range(TICKS):
         for j in range(CHUNKS):
             wait_halo_sent(t, j)
-            if t and j:
+            if passer_of(t, j, 0) is not None:
                 wait_forwarded(t, j)
-            state_copy(t + 1, j).wait_send()
+            if t + 1 < TICKS:
+                state_copy(t + 1, j).wait_send()
+            else:
+                home_copy(j, 0).wait_send()
+                home_copy(j, 1).wait_send()
 
 
 def per_device(nz, start_state, prior_path, wave_speed, kerr_coeff):
     any_space = pl.BlockSpec(memory_space=pl.ANY)
-    out = pl.pallas_call(
+    level = jax.ShapeDtypeStruct((4, ROWS, 128), jnp.float32)
+    previous, current = pl.pallas_call(
         functools.partial(kernel, nz),
-        out_shape=jax.ShapeDtypeStruct((2, 4, ROWS, 128), jnp.float32),
+        out_shape=(level, level),
         in_specs=[any_space] * 4,
-        out_specs=any_space,
+        out_specs=(any_space, any_space),
         scratch_shapes=[
             pltpu.VMEM((TICKS, 7, 4, ROWS + 2 * PAD, 128), jnp.float32),
             pltpu.VMEM((STEPS, 4, ROWS, 128), jnp.float32),
             pltpu.VMEM((2, TICKS * STEPS, 2, ROWS, 128), jnp.float32),
-            pltpu.VMEM((TICKS - 1, STEPS, 2, ROWS, 128), jnp.float32),
+            pltpu.VMEM((TICKS, STEPS, 2, ROWS, 128), jnp.float32),
             pltpu.VMEM((3, 4, ROWS, 128), jnp.float32),
             pltpu.VMEM((2, 4, ROWS, 128), jnp.float32),
             pltpu.SemaphoreType.DMA((TICKS, CHUNKS, 2)),
             pltpu.SemaphoreType.DMA((TICKS, CHUNKS, 2)),
+            pltpu.SemaphoreType.DMA((TICKS + 1, CHUNKS)),
+            pltpu.SemaphoreType.DMA((TICKS + 1, CHUNKS)),
             pltpu.SemaphoreType.DMA((TICKS, CHUNKS)),
             pltpu.SemaphoreType.DMA((TICKS, CHUNKS)),
-            pltpu.SemaphoreType.DMA((TICKS - 1, CHUNKS)),
-            pltpu.SemaphoreType.DMA((TICKS - 1, CHUNKS)),
             pltpu.SemaphoreType.DMA((4,)),
         ],
         compiler_params=pltpu.CompilerParams(
@@ -332,7 +355,7 @@
         ),
         name="relaxation",
     )(start_state[0], prior_path[0], wave_speed, kerr_coeff)
-    return out[None]
+    return jnp.stack([previous, current], 0)[None]
 
 
 def solution(mesh):

time: 78.9 us -> 77.5 us (0.982)
  local copies, waits for them, and re-layouts: 1.87 us -> 0 us
  other arithmetic: 0 us -> 1.86 us
  Pallas kernels: 76.9 us -> 75.5 us
    unnamed x1 -> x0, local copies, waits for them, and re-layouts: 1.87 us -> none
    broadcast_in_dim x0 -> x1, other arithmetic: none -> 1.86 us  [per_device(): return jnp.stack([previous, current], 0)[None]]
    pallas_call x1, Pallas kernels: 76.9 us -> 75.5 us  [per_device(): pl.pallas_call(functools.partial(kernel, nz), out_shape=(level, level), i...]
where the time goes in v5:
time: 77.5 us; the launch traced here: 77.4 us
  Pallas kernels  75.5 us (97%)
  other arithmetic  1.86 us (2%)
    pallas_call x1, Pallas kernels, per_device(): pl.pallas_call(functools.partial(kernel, nz), out_shape=(level, level), i...  75.5 us
    broadcast_in_dim x1, other arithmetic, per_device(): return jnp.stack([previous, current], 0)[None]  1.86 us

profile of v5, /device:TPU:1, one launch (start us, length us, event | category | flops | bytes accessed | tf_op | source)
XLA Modules:
  0.0 77.4 jit_solution(12798444730377304933)
XLA Ops:
  0.0 75.5 %relaxation.1 = (f32[4,128,128]{2,1,0:T(8,128)}, f32[4,128,128]{2,1,0:T(8,128)}) custom-call(f32[2,4,128,128]{3,2,1,0:T(8,128)} %bitcast.7, f32[5,4,128,128]{3,2,1,0:T(8,128)} %bitcast.6, f32[4,128,128]{2,1,0:T(8,128)} %speed.1, f32[4,128,128]{2,1,0:T(8,128)} %kerr.1), custom_call_target="tpu_custom_call" | custom-call | tf_op jit(solution)/shard_map/relaxation/pallas_call | solution.py:333
  75.5 1.9 %maximum_bitcast_fusion = f32[1,2,4,128,128]{4,3,2,1,0:T(8,128)} fusion(f32[1,4,128,128]{3,2,1,0:T(8,128)} %bitcast.9, f32[1,4,128,128]{3,2,1,0:T(8,128)} %bitcast.8), kind=kLoop, calls=%fused_computation | loop fusion | flops 131072 | bytes 1048576 | tf_op jit(solution)/shard_map/broadcast_in_dim | solution.py:358
